TPU v7x, 32 devices: a whole 2x2x4 slice. The times are simulated.
32 devices in a mesh: segment: 4 (over y, x), dp: 8 (over z, core).
Axes of the slice: x: 2, y: 2, z: 4, core: 2. Of those that a mesh axis runs over, the one named last changes fastest.
Arguments:
- input_tiles: bfloat16 [16, 1024, 276], P('dp'), may hold values from -6 to 6
- truth_fields: bfloat16 [16, 1024, 276], P('dp'), may hold values from -6 to 6
- horizon_group_label: int32 [16], P('dp'), may hold values from 0 to 2
- var_ids: int32 [69], replicated, may hold values from 0 to 68
- spectral_basis: float32 [256, 256], replicated, may hold values from -0.375 to 0.375
- embed_rows: float32 [349, 384], P(None, 'dp'), may hold values from -6 to 6
- qkv_weight: float32 [2, 384, 1152], P(None, 'dp'), may hold values from -0.3125 to 0.3125
- out_weight: float32 [2, 384, 384], P(None, 'dp'), may hold values from -1.25 to 1.25
- up_weight: float32 [2, 384, 1536], P(None, 'dp'), may hold values from -0.3125 to 0.3125
- down_weight: float32 [2, 1536, 384], P(None, None, 'dp'), may hold values from -0.15625 to 0.15625
- ada_weight: float32 [2, 384, 2304], P(None, 'dp'), may hold values from -0.3125 to 0.3125
- head_weight: float32 [384, 276], P('dp'), may hold values from -0.3125 to 0.3125
- embed_momentum: float32 [349, 384], P(None, 'dp'), may hold values from -2.3841858e-06 to 2.3841858e-06
- qkv_momentum: float32 [2, 384, 1152], P(None, 'dp'), may hold values from -2.3841858e-06 to 2.3841858e-06
- out_momentum: float32 [2, 384, 384], P(None, 'dp'), may hold values from -2.3841858e-06 to 2.3841858e-06
- up_momentum: float32 [2, 384, 1536], P(None, 'dp'), may hold values from -2.3841858e-06 to 2.3841858e-06
- down_momentum: float32 [2, 1536, 384], P(None, None, 'dp'), may hold values from -2.3841858e-06 to 2.3841858e-06
- ada_momentum: float32 [2, 384, 2304], P(None, 'dp'), may hold values from -2.3841858e-06 to 2.3841858e-06
- head_momentum: float32 [384, 276], P('dp'), may hold values from -2.3841858e-06 to 2.3841858e-06
- embed_average: float32 [349, 384], P(None, 'dp'), may hold values from -6 to 6
- qkv_average: float32 [2, 384, 1152], P(None, 'dp'), may hold values from -0.3125 to 0.3125
- out_average: float32 [2, 384, 384], P(None, 'dp'), may hold values from -1.25 to 1.25
- up_average: float32 [2, 384, 1536], P(None, 'dp'), may hold values from -0.3125 to 0.3125
- down_average: float32 [2, 1536, 384], P(None, None, 'dp'), may hold values from -0.15625 to 0.15625
- ada_average: float32 [2, 384, 2304], P(None, 'dp'), may hold values from -0.3125 to 0.3125
- head_average: float32 [384, 276], P('dp'), may hold values from -0.3125 to 0.3125
Outputs:
- loss_value: float32 [], replicated
- clip_norm: float32 [], replicated
- embed_next: float32 [349, 384], P(None, 'dp')
- qkv_next: float32 [2, 384, 1152], P(None, 'dp')
- out_next: float32 [2, 384, 384], P(None, 'dp')
- up_next: float32 [2, 384, 1536], P(None, 'dp')
- down_next: float32 [2, 1536, 384], P(None, None, 'dp')
- ada_next: float32 [2, 384, 2304], P(None, 'dp')
- head_next: float32 [384, 276], P('dp')
- embed_momentum_next: float32 [349, 384], P(None, 'dp')
- qkv_momentum_next: float32 [2, 384, 1152], P(None, 'dp')
- out_momentum_next: float32 [2, 384, 384], P(None, 'dp')
- up_momentum_next: float32 [2, 384, 1536], P(None, 'dp')
- down_momentum_next: float32 [2, 1536, 384], P(None, None, 'dp')
- ada_momentum_next: float32 [2, 384, 2304], P(None, 'dp')
- head_momentum_next: float32 [384, 276], P('dp')
- embed_average_next: float32 [349, 384], P(None, 'dp')
- qkv_average_next: float32 [2, 384, 1152], P(None, 'dp')
- out_average_next: float32 [2, 384, 384], P(None, 'dp')
- up_average_next: float32 [2, 384, 1536], P(None, 'dp')
- down_average_next: float32 [2, 1536, 384], P(None, None, 'dp')
- ada_average_next: float32 [2, 384, 2304], P(None, 'dp')
- head_average_next: float32 [384, 276], P('dp')
Inputs may be any that keep to these rules, and one draw needn't show every extreme that they name: `horizon_group_label`: 0 stands for 6 h, 1 for 12 h, 2 for 24 h.
All inputs are finite; a program needn't handle non-finite values.
Results may differ from a plain program's by a relative error of at most 0.012.
The roundings to bfloat16 on the way count: a program that leaves them out, or rounds other values in their place, can miss the bound.
Values may be sent and summed in bfloat16 or wider, within the bound.
No kernel may reach another device: no remote copies, remote signals or barrier semaphores. Data moves between devices by JAX's collectives and lax.ppermute only.
A program may use at most 192 MiB of HBM per device.

v0:
```python
import math

import jax
import jax.numpy as jnp
from jax import lax
from jax.experimental import pallas as pl
from jax.experimental.pallas import tpu as pltpu
from jax.sharding import Mesh, PartitionSpec as P

D = 384
HEADS = 6
HEAD_DIM = 64
FF = 1536
VARS = 69
CHANNELS = 69
LONP = 128
LATP = 8
LAYERS = 2
GROUPS = 3
PIXELS = 276
LEAD = PIXELS + VARS + 1
EROWS = LEAD + GROUPS
ECOLS = 512
EPS = 1e-06
CLIP = 0.001
KEEP = 0.9
BOOST = 20.0
LABEL_LANE = D - 1
HALF = FF // 2

F32 = jnp.float32
BF16 = jnp.bfloat16
CHIP = ("s", "z", "c")


def dot(a, b):
    return jnp.dot(a, b, preferred_element_type=F32)


def dot_nt(a, b):
    return lax.dot_general(a, b, (((1,), (1,)), ((), ())), preferred_element_type=F32)


def dot_tn(a, b):
    return lax.dot_general(a, b, (((0,), (0,)), ((), ())), preferred_element_type=F32)


def parts(x, count):
    out = []
    for step in range(count):
        piece = x.astype(BF16)
        out.append(piece)
        if step < count - 1:
            x = x - piece.astype(F32)
    return out


def normal(v):
    centered = v - jnp.mean(v, axis=-1, keepdims=True)
    inverse = lax.rsqrt(jnp.mean(centered * centered, axis=-1, keepdims=True) + EPS)
    return centered * inverse, inverse


def normal_back(d_x, x, inverse):
    return inverse * (
        d_x - jnp.mean(d_x, axis=-1, keepdims=True) - x * jnp.mean(d_x * x, axis=-1, keepdims=True)
    )


def lane_below(limit, shape):
    return lax.broadcasted_iota(jnp.int32, shape, len(shape) - 1) < limit


def sublane(shape):
    return lax.broadcasted_iota(jnp.int32, shape, 0)


def same_group():
    col = lax.broadcasted_iota(jnp.int32, (D, D), 1)
    return (sublane((D, D)) // 4 == col // 4).astype(BF16)


def chosen_table(vid_ref):
    return (sublane((ECOLS, D)) - PIXELS == vid_ref[...]).astype(BF16)


def first_of_four(shape):
    return sublane(shape) % 4 == 0


def cost(flops, size, exps=0):
    return pl.CostEstimate(flops=int(flops), bytes_accessed=int(size), transcendentals=int(exps))


VMEM = pl.BlockSpec(memory_space=pltpu.VMEM)
SMEM = pl.BlockSpec(memory_space=pltpu.SMEM)
ANY = pl.BlockSpec(memory_space=pl.ANY)
CHUNK = 256
AT_S, AT_Z, AT_C, AT_OWN, AT_LABEL = range(5)


def call(kernel, name, outs, inputs, estimate, scratch=(), limit=24, in_space=VMEM, out_spaces=None):
    return pl.pallas_call(
        kernel,
        in_specs=[SMEM] + [in_space] * (len(inputs) - 1),
        out_specs=out_spaces or [VMEM] * len(outs),
        out_shape=[jax.ShapeDtypeStruct(shape, kind) for shape, kind in outs],
        scratch_shapes=list(scratch),
        compiler_params=pltpu.CompilerParams(vmem_limit_bytes=limit << 20),
        cost_estimate=estimate,
        name=name,
    )(*inputs)


def rows_at(index, size):
    return pl.ds(pl.multiple_of(index * size, size), size)


def after(x, *others):
    return lax.optimization_barrier((x, others))[0]


def column_sum(v):
    return jnp.sum(v, axis=0, keepdims=True)


class Cut:
    def __init__(self, pairs, rows, split):
        self.pairs, self.rows, self.split = pairs, rows, split
        self.outputs = 2
        self.buffer = None

    def shapes(self, width, extra=False):
        if self.split:
            return [((4 * self.pairs + extra, self.rows, width), BF16)] * 2
        return [((4, D, width), BF16), ((1, 48, width), BF16)]

    def scratch(self, width):
        return [pltpu.VMEM((D, width), F32)]

    def on(self, buffer):
        other = Cut(self.pairs, self.rows, self.split)
        other.buffer = buffer
        return other

    def write(self, at_ref, outs, quarter, lane, value):
        width = value.shape[-1]
        cols = slice(lane, lane + width)
        if not self.split:
            outs[0][quarter, :, cols] = value.astype(BF16)
            return
        self.buffer[:, :width] = value
        core = at_ref[AT_C]
        for z in range(self.pairs):
            for ref, which in ((outs[0], core), (outs[1], 1 - core)):
                part = self.buffer[rows_at(2 * z + which, self.rows), :width]
                ref[quarter * self.pairs + z, :, cols] = part.astype(BF16)

    def write_extra(self, outs, value):
        value = value.astype(BF16)
        if self.split:
            outs[0][4 * self.pairs] = value
            outs[1][4 * self.pairs] = value
        else:
            outs[1][0] = value


def embed_kernel(
    at_ref, own_ref, got_ref, emb_ref, vid_ref,
    out_ref, agg_ref, x_ref, embk_ref, x_sc, bases_sc,
):
    tokens = own_ref.shape[1]
    half = tokens // 2
    emb = emb_ref[...]
    embk_ref[...] = emb.astype(F32).T.astype(BF16)
    query = jnp.broadcast_to(emb[:, LEAD - 1 : LEAD].astype(F32), (D, 128)).astype(BF16)
    by_row = dot_tn(emb, query)
    table = chosen_table(vid_ref)
    inside = sublane((D, 1)) < PIXELS
    proj = jnp.where(inside, by_row[:D, :1], 0.0)
    base = sum(dot_tn(table, p) for p in parts(by_row, 3))[:, :1]
    bases = dot_tn(table, embk_ref[...])
    bases_sc[...] = jnp.where(first_of_four((D, D)), bases, 0.0).astype(BF16)
    group = same_group()
    x_sc[...] = jnp.zeros_like(x_sc)
    x_sc[:PIXELS] = jnp.where(at_ref[AT_OWN] == 1, own_ref[...], got_ref[...])

    def step(i, carry):
        here = rows_at(i, CHUNK)
        source = lax.rem(i * CHUNK + at_ref[AT_C] * half, tokens)
        packed = x_sc[:, pl.ds(pl.multiple_of(source, CHUNK), CHUNK)]
        x = packed.astype(F32)
        scores = sum(dot(group, p) for p in parts(x * proj, 3)) + base
        scores = jnp.where(inside, scores * D ** (-0.5), -1e30)
        e = jnp.exp(scores - jnp.max(scores, axis=0, keepdims=True))
        agg = e * (4.0 / column_sum(e))

        @pl.when(i < half // CHUNK)
        def _():
            agg_ref[:, here] = agg
            x_ref[:, here] = packed

        total = dot_tn((agg * x).astype(BF16), embk_ref[:D])
        for p in parts(agg, 2):
            total = total + dot_tn(p, bases_sc[...])
        out_ref[here, :] = total.astype(BF16)
        return carry

    lax.fori_loop(0, tokens // CHUNK, step, 0)


def embed(at, own, got, emb, vid4):
    tokens = own.shape[1]
    return call(
        embed_kernel,
        "embed",
        [
            ((tokens, D), BF16),
            ((D, tokens // 2), F32),
            ((D, tokens // 2), BF16),
            ((ECOLS, D), BF16),
        ],
        [at, own, got, emb, vid4],
        cost(3e9, 4e6, 4e5),
        [pltpu.VMEM((D, tokens), BF16), pltpu.VMEM((D, D), BF16)],
    )


def embed_back(dh, x_ref, agg_ref, embk_ref, vid_ref):
    x = x_ref[...].astype(F32)
    agg = agg_ref[...]
    embk = embk_ref[:D]
    table = chosen_table(vid_ref)
    bases = dot_tn(table, embk_ref[...]).astype(BF16)
    query = embk_ref[LEAD - 1 : LEAD, :].astype(F32)
    g_patch = dot((agg * x).astype(BF16), dh)
    d_agg = dot_nt(bases, dh)
    group = same_group()
    for p in parts(dot_nt(embk, dh) * x, 2):
        d_agg = d_agg + dot(group, p)
    inner = 0.25 * column_sum(agg * d_agg)
    d_scores = agg * (d_agg - inner) * D ** (-0.5)
    d_proj = jnp.sum(d_scores * x, axis=-1, keepdims=True)
    d_base = jnp.sum(d_scores, axis=-1, keepdims=True)
    d_base = jnp.where(first_of_four(d_base.shape), d_base, 0.0)
    d_bases = d_base * query
    for p in parts(jnp.where(first_of_four((D, 1)), agg, 0.0), 2):
        d_bases = d_bases + dot(p, dh)
    g_table = sum(dot(table, p) for p in parts(d_bases, 2))
    d_query = column_sum(embk.astype(F32) * d_proj) + column_sum(bases.astype(F32) * d_base)
    total = g_table + jnp.where(sublane((ECOLS, 1)) == LEAD - 1, d_query, 0.0)
    return jnp.concatenate([total[:D] + g_patch + d_proj * query, total[D:]], axis=0)


def mod_row(mods_ref, at_ref, layer, index):
    row = layer * GROUPS + at_ref[AT_LABEL]
    return mods_ref[pl.ds(row, 1), D * index : D * (index + 1)]


def first_norm(h, mods_ref, at_ref, layer):
    x, inverse = normal(h.astype(F32))
    scale = 1.0 + mod_row(mods_ref, at_ref, layer, 1)
    return (x * scale + mod_row(mods_ref, at_ref, layer, 0)).astype(BF16), x, inverse


def pair_masks():
    low = lane_below(HEAD_DIM, (1, 128))
    return low, jnp.logical_not(low)


def both(own_ref, other_ref, lane):
    here = slice(lane, lane + 128)
    return jnp.concatenate([own_ref[:, here], other_ref[:, here]])


def attend(here, q_ref, own_ref, other_ref, att_ref, lse_ref):
    zero = jnp.zeros((), BF16)
    lane = lax.broadcasted_iota(jnp.int32, (CHUNK, 128), 1)
    sums = jnp.zeros((CHUNK, 128), F32)
    for pair in range(HEADS // 2):
        a = 128 * pair
        q = q_ref[here, a : a + 128] * 0.125
        keys = both(own_ref, other_ref, a)
        vals = both(own_ref, other_ref, D + a)
        mixed = jnp.zeros((CHUNK, 128), F32)
        for which, mask in enumerate(pair_masks()):
            scores = dot_nt(q, jnp.where(mask, keys, zero))
            top = jnp.max(scores, axis=-1, keepdims=True)
            e = jnp.exp(scores - top)
            total = jnp.sum(e, axis=-1, keepdims=True)
            mixed = mixed + dot(e.astype(BF16), jnp.where(mask, vals, zero)) * (1.0 / total)
            sums = jnp.where(lane == 2 * pair + which, top + jnp.log(total), sums)
        att_ref[here, a : a + 128] = mixed.astype(BF16)
    lse_ref[here, :] = sums


def gelu_and_slope(u):
    k = math.sqrt(2.0 / math.pi)
    t = jnp.tanh(k * (u + 0.044715 * (u * u * u)))
    cdf = 0.5 * (1.0 + t)
    return u * cdf, cdf + 0.5 * u * (1.0 - t * t) * k * (1.0 + 3 * 0.044715 * (u * u))


def feed_forward(here, h, one, mods_ref, at_ref, layer, w_ref, act_ref, slope_ref, n2_ref=None):
    middle = h.astype(F32) + mod_row(mods_ref, at_ref, layer, 2) * one
    x, _ = normal(middle)
    scale = 1.0 + mod_row(mods_ref, at_ref, layer, 4)
    n2 = (x * scale + mod_row(mods_ref, at_ref, layer, 3)).astype(BF16)
    if n2_ref is not None:
        n2_ref[here, :] = n2
    two = jnp.zeros((CHUNK, D), F32)
    for j in range(2):
        part = slice(HALF * j, HALF * (j + 1))
        act, slope = gelu_and_slope(dot(n2, w_ref[j, :, D : 3 * D]))
        slope_ref[here, part] = slope.astype(slope_ref.dtype)
        act = act.astype(BF16)
        act_ref[here, part] = act
        two = two + dot_nt(act, w_ref[2 + j, :, D : 3 * D])
    return middle, two, middle + mod_row(mods_ref, at_ref, layer, 5) * two


def feed_back(
    here, d_out, one, two, middle, slope_ref, mods_ref, at_ref, layer, w_ref,
    dunits_ref, dtwo_ref, done_ref, dmid_ref, datt_ref, dmod_ref, n2_ref=None,
):
    d_out = d_out.astype(F32)
    d_two = (mod_row(mods_ref, at_ref, layer, 5) * d_out).astype(BF16)
    dtwo_ref[here, :] = d_two
    d_n2 = jnp.zeros(d_out.shape, F32)
    for j in range(2):
        part = slice(HALF * j, HALF * (j + 1))
        slope = slope_ref[here, part].astype(F32)
        d_units = (slope * dot(d_two, w_ref[2 + j, :, D : 3 * D])).astype(BF16)
        dunits_ref[here, part] = d_units
        d_n2 = d_n2 + dot_nt(d_units, w_ref[j, :, D : 3 * D])
    x, inverse = normal(middle)
    scale = 1.0 + mod_row(mods_ref, at_ref, layer, 4)
    if n2_ref is not None:
        n2_ref[here, :] = (x * scale + mod_row(mods_ref, at_ref, layer, 3)).astype(BF16)
    d_mid = d_out + normal_back(d_n2 * scale, x, inverse)
    dmid_ref[here, :] = d_mid
    d_one = (mod_row(mods_ref, at_ref, layer, 2) * d_mid).astype(BF16)
    done_ref[here, :] = d_one
    datt_ref[here, :] = dot_nt(d_one, w_ref[3, :, :D]).astype(BF16)
    dmod_ref[2:3] += column_sum(d_mid * one)
    dmod_ref[3:4] += column_sum(d_n2)
    dmod_ref[4:5] += column_sum(d_n2 * x)
    dmod_ref[5:6] += column_sum(d_out * two)


def feed_gradients(at_ref, cut, outs, lane, n2_ref, dunits_ref, dtwo_ref, act_ref):
    for j in range(2):
        part = slice(HALF * j, HALF * (j + 1))
        cut.write(at_ref, outs, j, lane, dot_tn(n2_ref[...], dunits_ref[:, part]))
        cut.write(at_ref, outs, 2 + j, lane, dot_tn(dtwo_ref[...], act_ref[:, part]))


def rows_scratch(count, widths):
    return [pltpu.VMEM((count, width), BF16) for width in widths]


def block_kernel(
    at_ref, h_ref, mods_ref, w_ref,
    out_ref, q_out, own_out, other_out, att_out, lse_out, one_out, mid_out, slope_out, act_out, two_out,
    q_ref, own_ref, other_ref, att_ref, lse_ref, one_ref, mid_ref, slope_ref, act_ref, two_ref, sems,
):
    count = out_ref.shape[0]
    steps = count // CHUNK

    def project(i, carry):
        here = rows_at(i, CHUNK)
        normed, _, _ = first_norm(h_ref[here, :], mods_ref, at_ref, 0)
        q_ref[here, :] = dot(normed, w_ref[0, :, :D]).astype(BF16)
        for j in range(2):
            own_ref[here, D * j : D * (j + 1)] = dot(normed, w_ref[j + 1, :, :D]).astype(BF16)
        return carry

    lax.fori_loop(0, steps, project, 0)

    def project_other(i, carry):
        here = rows_at(i, CHUNK)
        normed, _, _ = first_norm(h_ref[rows_at(i + steps, CHUNK), :], mods_ref, at_ref, 0)
        for j in range(2):
            other_ref[here, D * j : D * (j + 1)] = dot(normed, w_ref[j + 1, :, :D]).astype(BF16)
        return carry

    lax.fori_loop(0, steps, project_other, 0)
    early = [
        pltpu.make_async_copy(ref, out, sems.at[2, i])
        for i, (ref, out) in enumerate(((q_ref, q_out), (own_ref, own_out), (other_ref, other_out)))
    ]
    for copy in early:
        copy.start()
    kept = (
        (att_ref, att_out), (lse_ref, lse_out), (one_ref, one_out), (mid_ref, mid_out),
        (slope_ref, slope_out), (act_ref, act_out), (two_ref, two_out),
    )

    def copies(i):
        here = rows_at(i, CHUNK)
        return [
            pltpu.make_async_copy(ref.at[here], out.at[here], sems.at[i, k])
            for k, (ref, out) in enumerate(kept)
        ]

    def step(i, carry):
        here = rows_at(i, CHUNK)
        attend(here, q_ref, own_ref, other_ref, att_ref, lse_ref)
        one = dot(att_ref[here, :], w_ref[3, :, :D])
        one_ref[here, :] = one.astype(BF16)
        middle, two, out = feed_forward(
            here, h_ref[here, :], one, mods_ref, at_ref, 0, w_ref, act_ref, slope_ref
        )
        mid_ref[here, :] = middle
        two_ref[here, :] = two.astype(BF16)
        out_ref[here, :] = out.astype(BF16)
        for copy in copies(i):
            copy.start()
        return carry

    lax.fori_loop(0, steps, step, 0)
    for copy in early:
        copy.wait()
    for i in range(steps):
        for copy in copies(i):
            copy.wait()


def block_forward(at, h, mods, weights):
    count = h.shape[0] // 2
    kept = [(D, BF16), (2 * D, BF16), (2 * D, BF16), (D, BF16), (128, F32), (D, BF16), (D, F32)]
    kept += [(FF, BF16), (FF, BF16), (D, BF16)]
    kept = [((count, width), kind) for width, kind in kept]
    return call(
        block_kernel,
        "block_forward",
        [((count, D), BF16)] + kept,
        [at, h, mods, weights],
        cost(6e9, 1.2e7, 3e6),
        [pltpu.VMEM(shape, kind) for shape, kind in kept] + [pltpu.SemaphoreType.DMA((3, 7))],
        limit=28,
        out_spaces=[VMEM] + [ANY] * len(kept),
    )


def qkv_kernel(at_ref, h_ref, mods_ref, w_ref, q_ref, kv_ref):
    def step(i, carry):
        here = rows_at(i, CHUNK)
        normed, _, _ = first_norm(h_ref[here, :], mods_ref, at_ref, 1)
        q_ref[here, :] = dot(normed, w_ref[0, :, :D]).astype(BF16)
        for j in range(2):
            kv_ref[here, D * j : D * (j + 1)] = dot(normed, w_ref[j + 1, :, :D]).astype(BF16)
        return carry

    lax.fori_loop(0, q_ref.shape[0] // CHUNK, step, 0)


def qkv_rows(at, h, mods, weights):
    count = h.shape[0]
    return call(
        qkv_kernel,
        "qkv_rows",
        [((count, D), BF16), ((count, 2 * D), BF16)],
        [at, h, mods, weights],
        cost(1e9, 3e6),
    )


def turn_kernel(
    at_ref, h_ref, q_ref, own_ref, other_ref, mods_ref, w_ref, truth_ref, got_ref, basis_ref,
    dmid_ref, datt_ref, att_ref, lse_ref, gout_ref, dmod_ref, loss_ref, keep_ref, send_ref,
    act_ref, dunits_ref, dtwo_ref, n2_ref, done_ref, flat_ref, dpred_ref, true_ref, slope_ref,
    basis_sc, buffer, *, seed, cut,
):
    count = h_ref.shape[0]
    outs = (keep_ref, send_ref)
    entries = LATP * CHANNELS * 2 * LONP
    dmod_ref[...] = jnp.zeros_like(dmod_ref)
    loss_ref[...] = jnp.zeros_like(loss_ref)
    row = lax.broadcasted_iota(jnp.int32, (PIXELS, 256), 0)
    col = lax.broadcasted_iota(jnp.int32, (PIXELS, 256), 1)
    lanes = rows_at(at_ref[AT_C], count)
    truth = jnp.where(at_ref[AT_OWN] == 1, truth_ref[:, lanes], got_ref[:, lanes])
    for b in range(2):
        picked = dot_tn(truth, (row == 2 * col + b).astype(BF16))
        true_ref[:, 256 * b : 256 * b + 256] = picked.astype(BF16)
    to = lax.broadcasted_iota(jnp.int32, (256, 256), 0)
    source = lax.broadcasted_iota(jnp.int32, (256, 256), 1)
    order = (source == 2 * (to % LONP) + to // LONP).astype(BF16)
    for i, p in enumerate(parts(basis_ref[...], 2)):
        basis_sc[i] = dot(order, p).astype(BF16)

    def step(i, carry):
        here = rows_at(i, CHUNK)
        attend(here, q_ref, own_ref, other_ref, att_ref, lse_ref)
        one = dot(att_ref[here, :], w_ref[3, :, :D])
        middle, two, h2 = feed_forward(
            here, h_ref[here, :], one, mods_ref, at_ref, 1, w_ref, act_ref, slope_ref, n2_ref
        )
        x, inverse = normal(h2.astype(BF16).astype(F32))
        flat = x.astype(BF16)
        flat_ref[here, :] = flat
        hw = [w_ref[j, :, 3 * D : 3 * D + 128] for j in range(4)]
        pred = [dot(flat, w) for w in hw]
        pred = [jnp.concatenate(pred[:2], axis=-1), jnp.concatenate(pred[2:], axis=-1)]
        hi, lo = basis_sc[0], basis_sc[1]
        grads = [[], []]
        loss = jnp.zeros((1, 1), F32)
        for p in range(CHUNK // LONP):
            part = slice(p * LONP, (p + 1) * LONP)
            fine = rows_at(i * (CHUNK // LONP) + p, LONP)
            seen = parts(jnp.concatenate([pred[0][part], pred[1][part]], axis=0), 2)
            waves = dot_tn(hi, seen[0]) + (dot_tn(hi, seen[1]) + dot_tn(lo, seen[0]))
            want = jnp.concatenate([true_ref[fine, :256], true_ref[fine, 256:]], axis=0)
            target = dot_tn(hi, want) + dot_tn(lo, want)
            top, low = waves[:LONP], waves[LONP:]
            gap = (top * top + low * low) - (
                target[:LONP] * target[:LONP] + target[LONP:] * target[LONP:]
            )
            loss = loss + jnp.sum(gap * gap, axis=(0, 1), keepdims=True)
            scaled = gap * (4.0 * seed / entries)
            d_waves = parts(jnp.concatenate([scaled * top, scaled * low], axis=0), 2)
            d_seen = dot(hi, d_waves[0]) + (dot(hi, d_waves[1]) + dot(lo, d_waves[0]))
            d_seen = d_seen.astype(BF16)
            grads[0].append(d_seen[:LONP])
            grads[1].append(d_seen[LONP:])
        loss_ref[...] += jnp.broadcast_to(loss * (seed / entries), loss_ref.shape)
        d_flat = jnp.zeros((CHUNK, D), F32)
        for b in range(2):
            whole = jnp.concatenate(grads[b], axis=0)
            dpred_ref[here, 256 * b : 256 * b + 256] = whole
            for j in range(2):
                d_flat = d_flat + dot_nt(whole[:, 128 * j : 128 * j + 128], hw[2 * b + j])
        d_h2 = normal_back(d_flat, x, inverse).astype(BF16)
        feed_back(
            here, d_h2, one, two, middle, slope_ref, mods_ref, at_ref, 1, w_ref,
            dunits_ref, dtwo_ref, done_ref, dmid_ref, datt_ref, dmod_ref,
        )
        return carry

    lax.fori_loop(0, count // CHUNK, step, 0)
    cut = cut.on(buffer)
    feed_gradients(at_ref, cut, outs, 0, n2_ref, dunits_ref, dtwo_ref, act_ref)
    for j in range(4):
        cut.write(at_ref, outs, j, HALF, dot_tn(flat_ref[...], dpred_ref[:, 128 * j : 128 * j + 128]))
    gout_ref[...] = dot_tn(att_ref[...], done_ref[...])


def turn(at, cut, h, q, own, other, mods, weights, truth, got, basis, seed):
    count = h.shape[0]
    return call(
        lambda *refs: turn_kernel(*refs, seed=seed, cut=cut),
        "turn",
        [
            ((count, D), F32),
            ((count, D), BF16),
            ((count, D), BF16),
            ((count, 128), F32),
            ((D, D), F32),
            ((8, D), F32),
            ((8, 128), F32),
        ]
        + cut.shapes(HALF + 128),
        [at, h, q, own, other, mods, weights, truth, got, basis],
        cost(1.2e10, 1.2e7, 4e6),
        rows_scratch(count, [FF, FF, D, D, D, D, 512, 512])
        + [pltpu.VMEM((count, FF), F32), pltpu.VMEM((2, 256, 256), BF16)]
        + cut.scratch(HALF),
        limit=32,
    )


def attention_back_kernel(
    at_ref, q_ref, own_ref, other_ref, lse_ref, att_ref, datt_ref, dq_ref, dk_ref, dv_ref, send_ref,
    dk_sc, dv_sc,
):
    zero = jnp.zeros((), BF16)
    count = q_ref.shape[0]
    dk_sc[...] = jnp.zeros_like(dk_sc)
    dv_sc[...] = jnp.zeros_like(dv_sc)

    def step(i, carry):
        rows = rows_at(i, CHUNK)
        for pair in range(HEADS // 2):
            a = 128 * pair
            here = slice(a, a + 128)
            q = q_ref[rows, here]
            d_att = datt_ref[rows, here]
            keys = both(own_ref, other_ref, a)
            vals = both(own_ref, other_ref, D + a)
            dots = d_att.astype(F32) * att_ref[rows, here].astype(F32)
            d_q = jnp.zeros((CHUNK, 128), F32)
            d_k = jnp.zeros((keys.shape[0], 128), F32)
            d_v = jnp.zeros((keys.shape[0], 128), F32)
            for which, mask in enumerate(pair_masks()):
                head = 2 * pair + which
                k = jnp.where(mask, keys, zero)
                v = jnp.where(mask, vals, zero)
                inner = jnp.sum(jnp.where(mask, dots, 0.0), axis=-1, keepdims=True)
                probs = jnp.exp(dot_nt(q * 0.125, k) - lse_ref[rows, head : head + 1])
                d_scores = (probs * (dot_nt(d_att, v) - inner)).astype(BF16)
                d_q = d_q + dot(d_scores, k)
                d_k = d_k + dot_tn(d_scores, jnp.where(mask, q, zero))
                d_v = d_v + dot_tn(probs.astype(BF16), jnp.where(mask, d_att, zero))
            dq_ref[rows, here] = (d_q * 0.125).astype(BF16)
            dk_sc[:, here] += d_k * 0.125
            dv_sc[:, here] += d_v
        return carry

    lax.fori_loop(0, count // CHUNK, step, 0)
    dk_ref[...] = dk_sc[:count]
    dv_ref[...] = dv_sc[:count]
    send_ref[0] = dk_sc[count:].astype(BF16)
    send_ref[1] = dv_sc[count:].astype(BF16)


def attention_back(at, q, own, other, lse, att, d_att):
    count = q.shape[0]
    return call(
        attention_back_kernel,
        "attention_back",
        [((count, D), BF16), ((count, D), F32), ((count, D), F32), ((2, count, D), BF16)],
        [at, q, own, other, lse, att, d_att],
        cost(6e9, 8e6, 3e6),
        [pltpu.VMEM((2 * count, D), F32)] * 2,
    )


def qkv_back(
    at_ref, cut, outs, lane, layer, dq_ref, dk_ref, dv_ref, got_ref, h_ref, dmid_ref, gout_ref, mods_ref, w_ref,
):
    count = dq_ref.shape[0]
    normed, x, inverse = first_norm(h_ref[:count], mods_ref, at_ref, layer)
    d_k = (dk_ref[...] + got_ref[0].astype(F32)).astype(BF16)
    d_v = (dv_ref[...] + got_ref[1].astype(F32)).astype(BF16)
    d_n = jnp.zeros((count, D), F32)
    for j, piece in enumerate((dq_ref[...], d_k, d_v)):
        d_n = d_n + dot_nt(piece, w_ref[j, :, :D])
        cut.write(at_ref, outs, j, lane, dot_tn(normed, piece))
    cut.write(at_ref, outs, 3, lane, gout_ref[...])
    scale = 1.0 + mod_row(mods_ref, at_ref, layer, 1)
    d_h = dmid_ref[...] + normal_back(d_n * scale, x, inverse)
    return d_h.astype(BF16), column_sum(d_n), column_sum(d_n * x)


def between_kernel(
    at_ref, dq_ref, dk_ref, dv_ref, got_ref, h_ref, dmid_ref, gout_ref, dmod_ref, mods_ref, w1_ref,
    one_ref, two_ref, mid_ref, slope_ref, act_ref, att_ref, w0_ref,
    dmid_out, datt_out, gout_out, dmod_out, dmod_next, keep_ref, send_ref,
    dh_sc, dunits_ref, dtwo_ref, n2_ref, done_ref, buffer, *, cut,
):
    outs = (keep_ref, send_ref)
    cut = cut.on(buffer)
    d_h, shift, scale = qkv_back(
        at_ref, cut, outs, 0, 1, dq_ref, dk_ref, dv_ref, got_ref, h_ref, dmid_ref, gout_ref, mods_ref, w1_ref,
    )
    dmod_out[...] = dmod_ref[...]
    dmod_out[0:1] = shift
    dmod_out[1:2] = scale
    dh_sc[...] = d_h
    dmod_next[...] = jnp.zeros_like(dmod_next)

    def step(i, carry):
        here = rows_at(i, CHUNK)
        feed_back(
            here, dh_sc[here, :], one_ref[here, :].astype(F32), two_ref[here, :].astype(F32),
            mid_ref[here, :], slope_ref, mods_ref, at_ref, 0, w0_ref,
            dunits_ref, dtwo_ref, done_ref, dmid_out, datt_out, dmod_next, n2_ref,
        )
        return carry

    lax.fori_loop(0, dh_sc.shape[0] // CHUNK, step, 0)
    feed_gradients(at_ref, cut, outs, D, n2_ref, dunits_ref, dtwo_ref, act_ref)
    gout_out[...] = dot_tn(att_ref[...], done_ref[...])


def between(at, cut, grads, h, d_mid, g_out, dmod, mods, w1, kept, w0):
    att, one, mid, slope, act, two = kept
    count = d_mid.shape[0]
    return call(
        lambda *refs: between_kernel(*refs, cut=cut),
        "between",
        [((count, D), F32), ((count, D), BF16), ((D, D), F32), ((8, D), F32), ((8, D), F32)]
        + cut.shapes(D + HALF),
        [at, *grads, h, d_mid, g_out, dmod, mods, w1, one, two, mid, slope, act, att, w0],
        cost(6e9, 2e7),
        rows_scratch(count, [D, FF, D, D, D]) + cut.scratch(HALF),
        limit=28,
    )


def last_kernel(
    at_ref, dq_ref, dk_ref, dv_ref, got_ref, h_ref, dmid_ref, gout_ref, dmod0_ref, dmod1_ref, loss_ref,
    mods_ref, w_ref, x_ref, agg_ref, embk_ref, vid_ref, keep_ref, send_ref, sums_sc, buffer, *, cut,
):
    outs = (keep_ref, send_ref)
    cut = cut.on(buffer)
    d_h, shift, scale = qkv_back(
        at_ref, cut, outs, 0, 0, dq_ref, dk_ref, dv_ref, got_ref, h_ref, dmid_ref, gout_ref, mods_ref, w_ref,
    )
    sums_sc[...] = jnp.zeros_like(sums_sc)
    for group in range(GROUPS):
        hot = (at_ref[AT_LABEL] == group).astype(F32)
        for layer, ref in enumerate((dmod0_ref, dmod1_ref)):
            at = 8 * (GROUPS * layer + group)
            sums_sc[at : at + 8, :D] = ref[...] * hot
        sums_sc[8 * group : 8 * group + 1, :D] = shift * hot
        sums_sc[8 * group + 1 : 8 * group + 2, :D] = scale * hot
    loss = loss_ref[0:1, 0:1]
    top = loss.astype(BF16).astype(F32)
    sums_sc[6:7, :] = jnp.broadcast_to(top, (1, ECOLS))
    sums_sc[7:8, :] = jnp.broadcast_to(loss - top, (1, ECOLS))
    cut.write_extra(outs, sums_sc[...])
    g = embed_back(d_h, x_ref, agg_ref, embk_ref, vid_ref).T
    for j in range(4):
        cut.write(at_ref, outs, j, D, g[:, 128 * j : 128 * j + 128])


def last(at, cut, grads, h, d_mid, g_out, dmod0, dmod1, loss, mods, w0, x, agg, embk, vid4):
    return call(
        lambda *refs: last_kernel(*refs, cut=cut),
        "last",
        cut.shapes(ECOLS, True),
        [at, *grads, h, d_mid, g_out, dmod0, dmod1, loss, mods, w0, x, agg, embk, vid4],
        cost(4e9, 1e7),
        [pltpu.VMEM((48, ECOLS), F32)] + cut.scratch(D),
        limit=28,
    )


def swap(x, axis, size, by):
    return lax.ppermute(x, axis, [(i, i ^ by) for i in range(size)])


def place_kernel(at_ref, *refs, columns, rows):
    out_ref, sems = refs[-2], refs[-1]
    inputs = refs[:-2]
    s, z, c = at_ref[AT_S], at_ref[AT_Z], at_ref[AT_C]
    copies = []
    index = 0
    for jc in range(2):
        for js in range(columns):
            source = inputs[jc * columns + js]
            for jz in range(source.shape[0]):
                at = rows_at((z ^ jz) * 2 + (c ^ jc), rows)
                target = out_ref.at[s ^ js, at] if columns > 1 else out_ref.at[at]
                copies.append(pltpu.make_async_copy(source.at[jz], target, sems.at[index]))
                index += 1
    for copy in copies:
        copy.start()
    for copy in copies:
        copy.wait()


def placed(at, own, got):
    columns, (zs, rows, width) = len(own), own[0].shape
    full = (zs * 2 * rows, width)
    shape = (columns,) + full if columns > 1 else full
    return call(
        lambda *refs: place_kernel(*refs, columns=columns, rows=rows),
        "placed",
        [(shape, BF16)],
        [at, *own, *got],
        cost(0, 4 * math.prod(shape)),
        [pltpu.SemaphoreType.DMA((2 * columns * zs,))],
        limit=4,
        in_space=ANY,
    )[0]


def two_rows(v):
    loss = v[6:7] + v[7:8]
    top = loss.astype(BF16).astype(F32)
    row = sublane(v.shape)
    return jnp.where(row == 6, top, jnp.where(row == 7, loss - top, v)).astype(BF16)


def add_core_kernel(at_ref, kept_ref, got_ref, own_ref, *sends):
    zs = 4
    for j in range(4):
        here = pl.ds((at_ref[AT_S] ^ j) * zs, zs)
        value = kept_ref[here].astype(F32) + got_ref[here].astype(F32)
        if j == 0:
            own_ref[:zs] = value
        else:
            sends[j - 1][:zs] = value.astype(BF16)
    if own_ref.shape[0] > zs:
        value = two_rows(kept_ref[4 * zs].astype(F32) + got_ref[4 * zs].astype(F32))
        own_ref[zs] = value.astype(F32)
        for send in sends:
            send[zs] = value


def summed(refs, at):
    a, b, c, d = (ref[at].astype(F32) for ref in refs)
    return (a + b) + (c + d)


def add_segment_kernel(at_ref, own_ref, a_ref, b_ref, c_ref, kept_ref, *sends):
    refs = (own_ref, a_ref, b_ref, c_ref)
    for j in range(4):
        value = summed(refs, at_ref[AT_Z] ^ j)
        if j == 0:
            kept_ref[0] = value
        else:
            sends[j - 1][0] = value.astype(BF16)
    if kept_ref.shape[0] > 1:
        value = two_rows(summed(refs, 4))
        kept_ref[1] = value.astype(F32)
        for send in sends:
            send[1] = value


def add_plane_kernel(at_ref, own_ref, a_ref, b_ref, c_ref, out_ref, *more):
    refs = (own_ref, a_ref, b_ref, c_ref)
    out_ref[...] = summed(refs, 0).astype(BF16)
    if more:
        more[0][...] = summed(refs, 1)


class Plain:
    split = False

    def __init__(self, sizes, at):
        self.sizes, self.at = sizes, at
        self.order = at.at[AT_S].set(0)

    def rows(self, x, ready):
        return lax.all_gather(x, ("z", "c"), axis=0, tiled=True)

    def columns(self, bundles, ready):
        return [lax.all_gather(x, ("z", "c"), axis=1, tiled=True) for x in bundles]

    def total(self, x):
        return lax.psum(x, ("z", "c"))

    def core(self, g):
        own = lax.psum_scatter(g[0].astype(F32), ("z", "c"), scatter_dimension=1, tiled=True)
        return lax.psum(own, "s"), lax.psum(g[1][0].astype(F32), CHIP)

    def segment(self, x):
        return x

    def plane(self, x):
        return x

    def shared(self, xs):
        return [[x[0][j].astype(BF16) for j in range(4)] for x in xs]


class Squares(Plain):
    split = True

    def __init__(self, sizes, at):
        self.sizes, self.at, self.order = sizes, at, at

    def across(self, x, axis):
        return [swap(x, axis, 4, by) for by in (1, 2, 3)]

    def rows(self, x, ready):
        own = jnp.stack([x] + self.across(x, "z"))
        return placed(self.at, [own], [swap(own, "c", 2, 1)])

    def columns(self, bundles, ready):
        out, wait = [], ()
        for x in bundles:
            mine = lax.dynamic_index_in_dim(x, self.at[AT_S], 0, keepdims=False)
            stack = jnp.stack([mine] + self.across(after(mine, *wait), "z"))
            own = [stack] + self.across(after(stack, *wait), "s")
            out.append((own, [swap(y, "c", 2, 1) for y in own]))
            wait = (stack,)
        return [placed(self.at, own, got) for own, got in out]

    def total(self, x):
        one, two, three = self.across(x, "z")
        x = (x + one) + (two + three)
        return x + swap(x, "c", 2, 1)

    def core(self, g):
        kept, sent = g
        count, rows, width = kept.shape
        full = (4 + count % 4, rows, width)
        return call(
            add_core_kernel, "add_core", [(full, F32)] + [(full, BF16)] * 3,
            [self.at, kept, swap(sent, "c", 2, 1)], cost(0, 8 * math.prod(kept.shape)),
        )

    def segment(self, x):
        own, *sends = x
        count, rows, width = own.shape
        one = (count - 3, rows, width)
        got = [swap(y, "s", 4, j + 1) for j, y in enumerate(sends)]
        return call(
            add_segment_kernel, "add_segment", [(one, F32)] + [(one, BF16)] * 3,
            [self.at, own, *got], cost(0, 12 * math.prod(own.shape)),
        )

    def plane(self, x):
        own, *sends = x
        count, rows, width = own.shape
        got = [swap(y, "z", 4, j + 1) for j, y in enumerate(sends)]
        return call(
            add_plane_kernel, "add_plane",
            [((rows, width), BF16)] + [((rows, width), F32)] * (count - 1),
            [self.at, own, *got], cost(0, 12 * math.prod(own.shape)),
        )

    def shared(self, xs):
        x = jnp.concatenate([y[0] for y in xs], axis=-1)
        pieces = [x] + self.across(x, "s")
        ends, at = [], 0
        for y in xs:
            width = y[0].shape[-1]
            ends.append([p[:, at : at + width] for p in pieces])
            at += width
        return ends


def lead_parts(emb_ref):
    lead = emb_ref[:, LEAD:EROWS].astype(BF16).astype(F32)
    gate = jax.nn.sigmoid(lead)
    return lead * gate, gate * (1.0 + lead * (1.0 - gate))


def ada_gradient(silu, sums_ref, layer, index):
    total = 0.0
    for group in range(GROUPS):
        at = 8 * (GROUPS * layer + group) + index
        total = total + silu[:, group : group + 1] * sums_ref[at : at + 1, :D]
    return total


def square_sum(v):
    return jnp.sum(v * v, axis=(0, 1), keepdims=True)


def gather_kernel(at_ref, *refs, widths):
    pieces, (emb_ref, ada_ref, sums_ref), outs = refs[:12], refs[12:15], refs[15:]
    ordered, (lead_ref, square_ref) = outs[:3], outs[3:]
    total = jnp.zeros((1, 1), F32)
    for k, ref in enumerate(ordered):
        squares = []
        for j in range(4):
            piece = pieces[4 * k + j][...]
            ref[at_ref[AT_S] ^ j] = piece
            squares.append(square_sum(piece.astype(F32)))
        total = total + ((squares[0] + squares[1]) + (squares[2] + squares[3]))
    silu, slope = lead_parts(emb_ref)
    rows = silu.shape[0]
    lane = lax.broadcasted_iota(jnp.int32, (rows, 128), 1)
    lead = jnp.zeros((rows, 128), F32)
    for group in range(GROUPS):
        d_silu = jnp.zeros((rows, 1), F32)
        for layer in range(LAYERS):
            for i in range(6):
                at = 8 * (GROUPS * layer + group) + i
                ada = ada_ref[layer, :, D * i : D * (i + 1)].astype(BF16).astype(F32)
                d_silu = d_silu + jnp.sum(ada * sums_ref[at : at + 1, :D], axis=-1, keepdims=True)
        value = d_silu * slope[:, group : group + 1]
        total = total + square_sum(value)
        lead = jnp.where(lane == group, value, lead)
    for layer in range(LAYERS):
        for i in range(6):
            total = total + square_sum(ada_gradient(silu, sums_ref, layer, i))
    lead_ref[...] = lead
    square_ref[...] = jnp.broadcast_to(total, square_ref.shape)


def gathered(at, pieces, emb_t, ada, sums):
    widths = [group[0].shape for group in pieces]
    return call(
        lambda *refs: gather_kernel(*refs, widths=widths),
        "gathered",
        [((4,) + shape, BF16) for shape in widths]
        + [((widths[0][0], 128), F32), ((8, 128), F32)],
        [at, *pieces[0], *pieces[1], *pieces[2], emb_t, ada, sums],
        cost(0, 4e6),
    )


def update_kernel(at_ref, *refs, rate):
    g1_ref, g2_ref, g3_ref, lead_ref, sums_ref, own_ref, got_ref = refs[:7]
    state = refs[7:28]
    outs, (loss_ref, norm_ref) = refs[28:49], refs[49:51]
    results, sems = refs[51:72], refs[72]
    squares = own_ref[0:1, 0:1] + got_ref[0:1, 0:1]
    norm = jnp.sqrt(squares)
    factor = CLIP / jnp.maximum(norm, CLIP)
    norm_ref[...] = norm
    loss_ref[...] = sums_ref[6:7, 0:1] + sums_ref[7:8, 0:1]
    silu, _ = lead_parts(state[0])
    rows = silu.shape[0]

    def advance(index, at, g):
        w_ref, m_ref, a_ref = (state[index + 7 * k] for k in range(3))
        g = g.astype(F32) * factor
        m = KEEP * m_ref[at] + g
        w = w_ref[at] - rate * (BOOST if index == 0 else 1.0) * (g + KEEP * m)
        results[index + 7][at] = m
        results[index][at] = w
        results[index + 14][at] = KEEP * a_ref[at] + (1.0 - KEEP) * w

    copies = []

    def send(index):
        for k in range(3):
            i = index + 7 * k
            copy = pltpu.make_async_copy(results[i], outs[i], sems.at[i])
            copy.start()
            copies.append(copy)

    every = slice(None)
    for layer in range(LAYERS):
        for i in range(6):
            g = ada_gradient(silu, sums_ref, layer, i)
            advance(5, (layer, every, slice(D * i, D * (i + 1))), g)
    send(5)
    att = (g3_ref, g2_ref)
    ff = ((g2_ref, D), (g1_ref, 0))
    for layer in range(LAYERS):
        ref, lane = ff[layer]
        for j in range(2):
            part = slice(HALF * j, HALF * (j + 1))
            advance(3, (layer, every, part), ref[j, :, lane : lane + HALF])
            advance(4, (layer, every, part), ref[2 + j, :, lane : lane + HALF])
    send(3)
    send(4)
    for layer in range(LAYERS):
        for j in range(3):
            advance(1, (layer, every, slice(D * j, D * (j + 1))), att[layer][j, :, :D])
    send(1)
    for layer in range(LAYERS):
        advance(2, (layer,), att[layer][3, :, :D])
    send(2)
    col = lax.broadcasted_iota(jnp.int32, (512, PIXELS), 1)
    row = lax.broadcasted_iota(jnp.int32, (512, PIXELS), 0)
    back = jnp.logical_and(row // 256 == col % 2, row % 256 == col // 2).astype(BF16)
    g_head = jnp.concatenate([g1_ref[j, :, HALF : HALF + 128] for j in range(4)], axis=-1)
    advance(6, (every,), dot(g_head, back))
    send(6)
    lane = lax.broadcasted_iota(jnp.int32, (rows, 128), 1)
    for j in range(3):
        g = g3_ref[j, :, D : D + 128].astype(F32)
        width = min(128, EROWS - 128 * j)
        if LEAD < 128 * j + width:
            first = LEAD - 128 * j
            for group in range(GROUPS):
                g = jnp.where(lane == first + group, lead_ref[:, group : group + 1], g)
        advance(0, (every, slice(128 * j, 128 * j + width)), g[:, :width])
    send(0)
    for copy in copies:
        copy.wait()


def updated(at, g, lead, sums, own, got, state, rate):
    shapes = [(x.shape, F32) for x in state]
    scalar = [((1, 1), F32)] * 2
    inputs = [at, *g, lead, sums, own, got, *state]
    return call(
        lambda *refs: update_kernel(*refs, rate=rate),
        "updated",
        shapes + scalar,
        inputs,
        cost(0, 2e7),
        [pltpu.VMEM(shape, kind) for shape, kind in shapes] + [pltpu.SemaphoreType.DMA((21,))],
        limit=24,
        out_spaces=[ANY] * 21 + [VMEM] * 2,
    )


def layer_bundle(qkv, out, up, down_t, extra):
    pieces = []
    for j in range(4):
        first = qkv[:, D * j : D * (j + 1)] if j < 3 else out
        source = up if j < 2 else down_t
        second = source[:, HALF * (j % 2) : HALF * (j % 2 + 1)]
        row = [first, second] + ([extra[j]] if extra is not None else [])
        pieces.append(jnp.concatenate(row, axis=-1))
    return jnp.stack(pieces)


def per_device(sizes, *arrays):
    (tiles_in, truth_in, labels, var_ids, basis) = arrays[:5]
    masters = arrays[5:12]
    embed_w, qkv_w, out_w, up_w, down_w, ada_w, head_w = masters
    segments, dp = sizes["s"], sizes["z"] * 2
    micro = tiles_in.shape[0]
    assert segments == 2 * micro
    rows = D // dp
    s, z, c = (lax.axis_index(name) for name in CHIP)
    which, owner = s % micro, s // micro
    is_owner = c == owner

    pairs = []
    for a in range(segments):
        for b in range(sizes["z"]):
            base = (a * sizes["z"] + b) * 2
            pairs.append((base + a // micro, base + 1 - a // micro))
    pick = lambda x: lax.dynamic_index_in_dim(x, which, 0, keepdims=False).T
    tiles, truth = pick(tiles_in), pick(truth_in)
    tiles_got = lax.ppermute(tiles, CHIP, pairs)
    label = jnp.where(is_owner, labels, lax.ppermute(labels, CHIP, pairs))
    label = lax.dynamic_index_in_dim(label, which, 0, keepdims=False)
    at = jnp.stack([s, z, c, is_owner, label]).astype(jnp.int32)
    move = (Squares if segments == 4 and sizes["z"] == 4 else Plain)(sizes, at)
    cut = Cut(sizes["z"], rows, move.split)

    emb_t = jnp.pad(embed_w.astype(BF16).T, ((0, 0), (0, ECOLS - EROWS)))
    down_t = down_w.astype(BF16).transpose(0, 2, 1)
    wide = jnp.arange(512)
    source = 2 * (wide % 256) + wide // 256
    to_head = (jnp.arange(PIXELS)[:, None] == source[None]) & (wide % 256 < PIXELS // 2)[None]
    head_b = dot(head_w.astype(BF16), to_head.astype(BF16)).astype(BF16)
    head_b = [head_b[:, 128 * j : 128 * j + 128] for j in range(4)]
    qkv_b, out_b, up_b = qkv_w.astype(BF16), out_w.astype(BF16), up_w.astype(BF16)
    bundles = [
        layer_bundle(qkv_b[l], out_b[l], up_b[l], down_t[l], head_b if l == 1 else None)
        for l in range(LAYERS)
    ]

    emb = move.rows(emb_t, ())
    w0, w1 = move.columns(bundles, ())

    lead = embed_w[LEAD:].astype(BF16).astype(F32)
    ada = ada_w.astype(BF16).astype(F32)
    mods = jnp.einsum("gd,ldm->lgm", jax.nn.silu(lead), ada, precision=lax.Precision.HIGHEST)
    mods = jnp.pad(mods.reshape(LAYERS * GROUPS, 6 * D), ((0, 2), (0, 0)))
    mods = move.total(mods)

    vid4 = jnp.pad(jnp.repeat(var_ids, 4), (0, D - PIXELS), constant_values=-1)[None].astype(
        jnp.int32
    )
    h0, agg, x_own, embk = embed(at, tiles, tiles_got, emb, vid4)
    h1, q0, own0, other0, att0, lse0, *kept = block_forward(at, h0, mods, w0)
    q1, own1 = qkv_rows(at, h1, mods, w1)
    other1 = swap(own1, "c", 2, 1)
    truth_got = lax.ppermute(after(truth, emb), CHIP, pairs)
    d_mid, d_att, att1, lse1, g_out, dmod1, loss, *g_first = turn(
        at, cut, h1, q1, own1, other1, mods, w1, truth, truth_got, basis, 1.0 / (micro * dp)
    )

    def attention_grads(at, q, own, other, lse, att, d_att):
        d_q, d_k, d_v, send = attention_back(at, q, own, other, lse, att, d_att)
        return d_q, d_k, d_v, swap(send, "c", 2, 1)

    grads = attention_grads(at, q1, own1, other1, lse1, att1, d_att)
    first = move.core(g_first)
    d_mid, d_att, g_out, dmod1, dmod0, *g_second = between(
        after(at, *first), cut, grads, h1, d_mid, g_out, dmod1, mods, w1, [att0, *kept], w0
    )
    grads = attention_grads(at, q0, own0, other0, lse0, att0, d_att)
    second = move.core(g_second)
    first = move.segment(first)
    g_third = last(
        after(at, *second, *first), cut, grads, h0, d_mid, g_out, dmod0, dmod1, loss, mods, w0, x_own, agg, embk, vid4
    )
    third = move.core(g_third)
    first = move.plane(first)
    second = move.plane(move.segment(second))
    third = move.plane(move.segment(third))
    ends = move.shared([first, second]) + move.shared([third])
    sums = third[1]

    views = []
    for k in range(3):
        w = list(arrays[5 + 7 * k : 12 + 7 * k])
        w[0], w[4] = w[0].T, w[4].transpose(0, 2, 1)
        views += w
    g1, g2, g3, lead_g, squares = gathered(move.order, ends, views[0], views[5], sums)
    if move.split:
        one, two, three = move.across(squares, "z")
        own = (squares + one) + (two + three)
        got = swap(own, "c", 2, 1)
    else:
        own, got = move.total(squares), jnp.zeros_like(squares)
    count = sum(w.size for w in masters) * dp
    rate = 0.02 * math.sqrt(count) / CLIP
    *new, loss_value, norm = updated(at, (g1, g2, g3), lead_g, sums, own, got, views, rate)
    for k in range(3):
        new[7 * k] = new[7 * k].T
        new[7 * k + 4] = new[7 * k + 4].transpose(0, 2, 1)
    return (loss_value.reshape(()), norm.reshape(()), *new)


def solution(mesh):
    segments, dp = mesh.shape["segment"], mesh.shape["dp"]
    sizes = {"s": segments, "z": dp // 2, "c": 2}
    split = Mesh(mesh.devices.reshape(segments, dp // 2, 2), CHIP)
    d = ("z", "c")
    weights = (
        P(None, d),
        P(None, d, None),
        P(None, d, None),
        P(None, d, None),
        P(None, None, d),
        P(None, d, None),
        P(d, None),
    )
    return jax.shard_map(
        lambda *arrays: per_device(sizes, *arrays),
        mesh=split,
        in_specs=(P(d, None, None), P(d, None, None), P(d), P(), P()) + weights * 3,
        out_specs=(P(), P()) + weights * 3,
        check_vma=False,
    )
```

profile of v0, /device:TPU:0, one launch (start us, length us, event | category | flops | bytes accessed | tf_op | source)
XLA Modules:
  0.0 288.6 jit_solution(1204181956893465018)
XLA Ops:
  2.3 5.0 %collective-permute-start.4 = (bf16[48,512]{1,0:T(8,128)(2,1)}, bf16[48,512]{1,0:T(8,128)(2,1)}, u32[]{:S(2)}, u32[]{:S(2)}) collective-permute-start(bf16[48,512]{1,0:T(8,128)(2,1)} %get-tuple-element.254), channel_id=1, source_target_pairs={{0,6},{2,4},{4,2},{6,0},{1,7},{3,5},{5,3},{7,1},{8,14},{10,12},{12... | collective-permute-start | bytes 147464 | tf_op jit(solution)/shard_map/ppermute | solution.py:732
  30.2 2.9 %collective-permute-start.6 = (f32[8,2304]{1,0:T(8,128)}, f32[8,2304]{1,0:T(8,128)S(1)}, u32[]{:S(2)}, u32[]{:S(2)}) collective-permute-start(f32[8,2304]{1,0:T(8,128)} %pad.14), channel_id=1, source_target_pairs={{0,2},{2,0},{4,6},{6,4},{1,3},{3,1},{5,7},{7,5},{8,10},{10,8},{12,... | collective-permute-start | bytes 221192 | tf_op jit(solution)/shard_map/ppermute | solution.py:732
  49.1 3.1 %collective-permute-start.14 = (bf16[4,48,1152]{2,1,0:T(8,128)(2,1)S(1)}, bf16[4,48,1152]{2,1,0:T(8,128)(2,1)}, u32[]{:S(2)}, u32[]{:S(2)}) collective-permute-start(bf16[4,48,1152]{2,1,0:T(8,128)(2,1)S(1)} %pad_maximum_fusion.1.refs_1_), channel_id=1, source_target_pairs={{0,16},{8,24},{16,0},{24,8},{1,17},{9,25},{17,1},{25,9},{2,18},{10... | collective-permute-start | bytes 1327112 | tf_op jit(solution)/shard_map/ppermute | solution.py:732
  54.9 16.2 %collective-permute-done.14.refs_3_ = bf16[4,48,1152]{2,1,0:T(8,128)(2,1)} collective-permute-done((bf16[4,48,1152]{2,1,0:T(8,128)(2,1)S(1)}, bf16[4,48,1152]{2,1,0:T(8,128)(2,1)}, u32[]{:S(2)}, u32[]{:S(2)}) %collective-permute-start.14) | collective-permute-done | bytes 442400 | tf_op jit(solution)/shard_map/ppermute | solution.py:732
  80.5 9.4 %embed.1 = (bf16[1024,384]{1,0:T(8,128)(2,1)S(1)}, f32[384,512]{1,0:T(8,128)S(1)}, bf16[384,512]{1,0:T(8,128)(2,1)S(1)}, bf16[512,384]{1,0:T(8,128)(2,1)S(1)}) custom-call(s32[5]{0:T(128)S(1)} %stack.95.refs_0_.at_ref, bf16[276,1024]{1,0:T(8,128)(2,1)S(1)} %bitcast.90, bf16[276,1024]{1,0:T(8,128)(2,1)} %collective-permute-done.1.got_ref, ...), custom_call_target="tpu_custom_call" | custom-call | flops 3000000000 | bytes 4000000 | tf_op jit(solution)/shard_map/embed/pallas_call | solution.py:103
  89.9 4.8 %collective-permute-done.24.refs_3_ = bf16[4,48,1280]{2,1,0:T(8,128)(2,1)} collective-permute-done((bf16[4,48,1280]{2,1,0:T(8,128)(2,1)S(1)}, bf16[4,48,1280]{2,1,0:T(8,128)(2,1)}, u32[]{:S(2)}, u32[]{:S(2)}) %collective-permute-start.24) | collective-permute-done | bytes 491552 | tf_op jit(solution)/shard_map/ppermute | solution.py:732
  95.7 3.3 %placed.4.w_ref.refs_17_.refs_12_ = bf16[4,384,1152]{2,1,0:T(8,128)(2,1)S(1)} custom-call(s32[5]{0:T(128)S(1)} %stack.95.refs_0_.at_ref, bf16[4,48,1152]{2,1,0:T(8,128)(2,1)S(1)} %pad_maximum_fusion.1.refs_1_, bf16[4,48,1152]{2,1,0:T(8,128)(2,1)} %collective-permute-done.13.refs_2_, bf16[4,48,1152]{2,1,0:T(8,128)(2,1)} %collective-permute-done.14.refs_3_, ...), custom_call_target="tpu_custom_call" | custom-call | bytes 7077888 | tf_op jit(solution)/shard_map/placed/pallas_call | solution.py:103
  99.0 16.2 %block_forward.1 = (bf16[512,384]{1,0:T(8,128)(2,1)S(1)}, bf16[512,384]{1,0:T(8,128)(2,1)S(1)}, bf16[512,768]{1,0:T(8,128)(2,1)S(1)}, bf16[512,768]{1,0:T(8,128)...) custom-call(s32[5]{0:T(128)S(1)} %stack.95.refs_0_.at_ref, ...), custom_call_target="tpu_custom_call" | custom-call | flops 6000000000 | bytes 12000000 | tf_op jit(solution)/shard_map/block_forward/pallas_call | solution.py:103
  115.4 4.6 %placed.5.w_ref.refs_6_.refs_10_ = bf16[4,384,1280]{2,1,0:T(8,128)(2,1)S(1)} custom-call(s32[5]{0:T(128)S(1)} %stack.95.refs_0_.at_ref, bf16[4,48,1280]{2,1,0:T(8,128)(2,1)S(1)} %pad_maximum_fusion.refs_1_, bf16[4,48,1280]{2,1,0:T(8,128)(2,1)} %collective-permute-done.23.refs_2_, bf16[4,48,1280]{2,1,0:T(8,128)(2,1)} %collective-permute-done.24.refs_3_, ...), custom_call_target="tpu_custom_call" | custom-call | bytes 7864320 | tf_op jit(solution)/shard_map/placed/pallas_call | solution.py:103
  127.5 20.2 %turn.1 = (f32[512,384]{1,0:T(8,128)S(1)}, bf16[512,384]{1,0:T(8,128)(2,1)S(1)}, bf16[512,384]{1,0:T(8,128)(2,1)S(1)}, f32[512,128]{1,0:T(8,128)S(1)}, f32[384,3...) custom-call(s32[5]{0:T(128)S(1)} %stack.95.refs_0_.at_ref, ...), custom_call_target="tpu_custom_call" | custom-call | flops 12000000000 | bytes 12000000 | tf_op jit(solution)/shard_map/turn/pallas_call | solution.py:103
  148.2 10.6 %attention_back.2 = (bf16[512,384]{1,0:T(8,128)(2,1)S(1)}, f32[512,384]{1,0:T(8,128)S(1)}, f32[512,384]{1,0:T(8,128)S(1)}, bf16[2,512,384]{2,1,0:T(8,128)(2,1)S(1)}) custom-call(s32[5]{0:T(128)S(1)} %stack.95.refs_0_.at_ref, bf16[512,384]{1,0:T(8,128)(2,1)S(1)} %get-tuple-element.129.refs_2_.q_ref, bf16[512,768]{1,0:T(8,128)(2,1)S(1)} %get-tuple-element.130.refs_3_.own_ref, ...), custom_call_target="tpu_custom_call" | custom-call | flops 6000000000 | bytes 8000000 | tf_op jit(solution)/shard_map/attention_back/pallas_call | solution.py:103
  161.2 7.1 %between.1 = (f32[512,384]{1,0:T(8,128)S(1)}, bf16[512,384]{1,0:T(8,128)(2,1)S(1)}, f32[384,384]{1,0:T(8,128)S(1)}, f32[8,384]{1,0:T(8,128)S(1)}, f32[8,384]{1,0...) custom-call(s32[5]{0:T(128)S(1)} %stack.95.refs_0_.at_ref, ...), custom_call_target="tpu_custom_call" | custom-call | flops 6000000000 | bytes 20000000 | tf_op jit(solution)/shard_map/between/pallas_call | solution.py:103
  168.5 10.8 %attention_back.3 = (bf16[512,384]{1,0:T(8,128)(2,1)S(1)}, f32[512,384]{1,0:T(8,128)S(1)}, f32[512,384]{1,0:T(8,128)S(1)}, bf16[2,512,384]{2,1,0:T(8,128)(2,1)S(1)}) custom-call(s32[5]{0:T(128)S(1)} %stack.95.refs_0_.at_ref, bf16[512,384]{1,0:T(8,128)(2,1)S(1)} %copy-done.37, bf16[512,768]{1,0:T(8,128)(2,1)S(1)} %copy-done.33, ...), custom_call_target="tpu_custom_call" | custom-call | flops 6000000000 | bytes 8000000 | tf_op jit(solution)/shard_map/attention_back/pallas_call | solution.py:103
  183.2 7.4 %collective-permute-done.33.a_ref = bf16[4,48,896]{2,1,0:T(8,128)(2,1)S(1)} collective-permute-done((bf16[4,48,896]{2,1,0:T(8,128)(2,1)S(1)}, bf16[4,48,896]{2,1,0:T(8,128)(2,1)S(1)}, u32[]{:S(2)}, u32[]{:S(2)}) %collective-permute-start.33) | collective-permute-done | bytes 344096 | tf_op jit(solution)/shard_map/ppermute | solution.py:732
  190.6 8.1 %collective-permute-done.34.b_ref = bf16[4,48,896]{2,1,0:T(8,128)(2,1)S(1)} collective-permute-done((bf16[4,48,896]{2,1,0:T(8,128)(2,1)S(1)}, bf16[4,48,896]{2,1,0:T(8,128)(2,1)S(1)}, u32[]{:S(2)}, u32[]{:S(2)}) %collective-permute-start.34) | collective-permute-done | bytes 344096 | tf_op jit(solution)/shard_map/ppermute | solution.py:732
  200.8 5.4 %last.1 = (bf16[17,48,512]{2,1,0:T(8,128)(2,1)S(1)}, bf16[17,48,512]{2,1,0:T(8,128)(2,1)S(1)}) custom-call(s32[5]{0:T(128)S(1)} %stack.95.refs_0_.at_ref, bf16[512,384]{1,0:T(8,128)(2,1)S(1)} %get-tuple-element.175.refs_1_, f32[512,384]{1,0:T(8,128)S(1)} %get-tuple-element.176.refs_2_, f32[512,384]{1,0:T(8,128)S(1)} %get-tuple-element.177.refs_3_, ...), custom_call_target="tpu_custom_call" | custom-call | flops 4000000000 | bytes 10000000 | tf_op jit(solution)/shard_map/last/pallas_call | solution.py:103
  213.5 5.8 %collective-permute-done.41.a_ref = bf16[4,48,1152]{2,1,0:T(8,128)(2,1)S(1)} collective-permute-done((bf16[4,48,1152]{2,1,0:T(8,128)(2,1)S(1)}, bf16[4,48,1152]{2,1,0:T(8,128)(2,1)S(1)}, u32[]{:S(2)}, u32[]{:S(2)}) %collective-permute-start.41) | collective-permute-done | bytes 442400 | tf_op jit(solution)/shard_map/ppermute | solution.py:732
  220.7 9.1 %collective-permute-start.53 = (bf16[5,48,512]{2,1,0:T(8,128)(2,1)S(1)}, bf16[5,48,512]{2,1,0:T(8,128)(2,1)S(1)}, u32[]{:S(2)}, u32[]{:S(2)}) collective-permute-start(bf16[5,48,512]{2,1,0:T(8,128)(2,1)S(1)} %get-tuple-element.191), channel_id=1, source_target_pairs={{0,16},{8,24},{16,0},{24,8},{1,17},{9,25},{17,1},{25,9},{2,18},{10... | collective-permute-start | bytes 737288 | tf_op jit(solution)/shard_map/ppermute | solution.py:732
  235.0 4.4 %collective-permute-done.38.c_ref = bf16[1,48,896]{2,1,0:T(8,128)(2,1)S(1)} collective-permute-done((bf16[1,48,896]{2,1,0:T(8,128)(2,1)S(1)}, bf16[1,48,896]{2,1,0:T(8,128)(2,1)S(1)}, u32[]{:S(2)}, u32[]{:S(2)}) %collective-permute-start.38) | collective-permute-done | bytes 86048 | tf_op jit(solution)/shard_map/ppermute | solution.py:732
  243.0 5.1 %collective-permute-done.45.b_ref = bf16[1,48,1152]{2,1,0:T(8,128)(2,1)S(1)} collective-permute-done((bf16[1,48,1152]{2,1,0:T(8,128)(2,1)S(1)}, bf16[1,48,1152]{2,1,0:T(8,128)(2,1)S(1)}, u32[]{:S(2)}, u32[]{:S(2)}) %collective-permute-start.45) | collective-permute-done | bytes 110624 | tf_op jit(solution)/shard_map/ppermute | solution.py:732
  261.5 2.9 collective-permute-done.57.c_ref
  270.1 2.9 %collective-permute-done.60.refs_12_ = bf16[48,512]{1,0:T(8,128)(2,1)S(1)} collective-permute-done((bf16[48,512]{1,0:T(8,128)(2,1)S(1)}, bf16[48,512]{1,0:T(8,128)(2,1)S(1)}, u32[]{:S(2)}, u32[]{:S(2)}) %collective-permute-start.60) | collective-permute-done | bytes 49184 | tf_op jit(solution)/shard_map/ppermute | solution.py:732
  274.9 2.8 collective-permute-start.63
  282.7 5.5 %updated.1 = (f32[48,349]{1,0:T(8,128)}, f32[2,48,1152]{2,1,0:T(8,128)}, f32[2,48,384]{2,1,0:T(8,128)}, f32[2,48,1536]{2,1,0:T(8,128)}, f32[2,48,1536]{2,1,0:T(8...) custom-call(s32[5]{0:T(128)S(1)} %stack.95.refs_0_.at_ref, ...), custom_call_target="tpu_custom_call" | custom-call | bytes 20000000 | tf_op jit(solution)/shard_map/updated/pallas_call | solution.py:103
  (289 shorter events, 112.7 us)
Async XLA Ops:
  2.3 19.9 %collective-permute-start.4 = (bf16[48,512]{1,0:T(8,128)(2,1)}, bf16[48,512]{1,0:T(8,128)(2,1)}, u32[]{:S(2)}, u32[]{:S(2)}) collective-permute-start(bf16[48,512]{1,0:T(8,128)(2,1)} %get-tuple-element.254), channel_id=1, source_target_pairs={{0,6},{2,4},{4,2},{6,0},{1,7},{3,5},{5,3},{7,1},{8,14},{10,12},{12... | collective-permute-start | bytes 147464 | tf_op jit(solution)/shard_map/ppermute | solution.py:732
  11.2 26.4 %collective-permute-start.7 = (f32[8,2304]{1,0:T(8,128)}, f32[8,2304]{1,0:T(8,128)}, u32[]{:S(2)}, u32[]{:S(2)}) collective-permute-start(f32[8,2304]{1,0:T(8,128)} %pad.14), channel_id=1, source_target_pairs={{0,4},{2,6},{4,0},{6,2},{1,5},{3,7},{5,1},{7,3},{8,12},{10,14},{12... | collective-permute-start | bytes 221192 | tf_op jit(solution)/shard_map/ppermute | solution.py:732
  13.6 24.0 %collective-permute-start.8 = (f32[8,2304]{1,0:T(8,128)}, f32[8,2304]{1,0:T(8,128)}, u32[]{:S(2)}, u32[]{:S(2)}) collective-permute-start(f32[8,2304]{1,0:T(8,128)} %pad.14), channel_id=1, source_target_pairs={{0,6},{2,4},{4,2},{6,0},{1,7},{3,5},{5,3},{7,1},{8,14},{10,12},{12... | collective-permute-start | bytes 221192 | tf_op jit(solution)/shard_map/ppermute | solution.py:732
  43.3 31.2 %collective-permute-start.1 = (bf16[276,1024]{1,0:T(8,128)(2,1)S(1)}, bf16[276,1024]{1,0:T(8,128)(2,1)}, u32[]{:S(2)}, u32[]{:S(2)}) collective-permute-start(bf16[276,1024]{1,0:T(8,128)(2,1)S(1)} %bitcast.89), channel_id=1, source_target_pairs={{0,1},{2,3},{4,5},{6,7},{8,9},{10,11},{12,13},{14,15},{17,16},{19,... | collective-permute-start | bytes 1695752 | tf_op jit(solution)/shard_map/ppermute | solution.py:1101
  47.6 27.4 %collective-permute-start.23 = (bf16[4,48,1280]{2,1,0:T(8,128)(2,1)S(1)}, bf16[4,48,1280]{2,1,0:T(8,128)(2,1)}, u32[]{:S(2)}, u32[]{:S(2)}) collective-permute-start(bf16[4,48,1280]{2,1,0:T(8,128)(2,1)S(1)} %pad_maximum_fusion.refs_1_), channel_id=1, source_target_pairs={{0,8},{8,0},{16,24},{24,16},{1,9},{9,1},{17,25},{25,17},{2,10},{10... | collective-permute-start | bytes 1474568 | tf_op jit(solution)/shard_map/ppermute | solution.py:732
  49.1 22.0 %collective-permute-start.14 = (bf16[4,48,1152]{2,1,0:T(8,128)(2,1)S(1)}, bf16[4,48,1152]{2,1,0:T(8,128)(2,1)}, u32[]{:S(2)}, u32[]{:S(2)}) collective-permute-start(bf16[4,48,1152]{2,1,0:T(8,128)(2,1)S(1)} %pad_maximum_fusion.1.refs_1_), channel_id=1, source_target_pairs={{0,16},{8,24},{16,0},{24,8},{1,17},{9,25},{17,1},{25,9},{2,18},{10... | collective-permute-start | bytes 1327112 | tf_op jit(solution)/shard_map/ppermute | solution.py:732
  52.9 20.8 %collective-permute-start.15 = (bf16[4,48,1152]{2,1,0:T(8,128)(2,1)S(1)}, bf16[4,48,1152]{2,1,0:T(8,128)(2,1)}, u32[]{:S(2)}, u32[]{:S(2)}) collective-permute-start(bf16[4,48,1152]{2,1,0:T(8,128)(2,1)S(1)} %pad_maximum_fusion.1.refs_1_), channel_id=1, source_target_pairs={{0,24},{8,16},{16,8},{24,0},{1,25},{9,17},{17,9},{25,1},{2,26},{10... | collective-permute-start | bytes 1327112 | tf_op jit(solution)/shard_map/ppermute | solution.py:732
  53.2 21.2 %collective-permute-start.16 = (bf16[4,48,1152]{2,1,0:T(8,128)(2,1)S(1)}, bf16[4,48,1152]{2,1,0:T(8,128)(2,1)}, u32[]{:S(2)}, u32[]{:S(2)}) collective-permute-start(bf16[4,48,1152]{2,1,0:T(8,128)(2,1)S(1)} %pad_maximum_fusion.1.refs_1_), channel_id=1, source_target_pairs={{0,1},{1,0},{2,3},{3,2},{4,5},{5,4},{6,7},{7,6},{8,9},{9,8},{10,11... | collective-permute-start | bytes 1327112 | tf_op jit(solution)/shard_map/ppermute | solution.py:732
  71.1 23.6 %collective-permute-start.24 = (bf16[4,48,1280]{2,1,0:T(8,128)(2,1)S(1)}, bf16[4,48,1280]{2,1,0:T(8,128)(2,1)}, u32[]{:S(2)}, u32[]{:S(2)}) collective-permute-start(bf16[4,48,1280]{2,1,0:T(8,128)(2,1)S(1)} %pad_maximum_fusion.refs_1_), channel_id=1, source_target_pairs={{0,16},{8,24},{16,0},{24,8},{1,17},{9,25},{17,1},{25,9},{2,18},{10... | collective-permute-start | bytes 1474568 | tf_op jit(solution)/shard_map/ppermute | solution.py:732
  73.7 21.0 %collective-permute-start.25 = (bf16[4,48,1280]{2,1,0:T(8,128)(2,1)S(1)}, bf16[4,48,1280]{2,1,0:T(8,128)(2,1)}, u32[]{:S(2)}, u32[]{:S(2)}) collective-permute-start(bf16[4,48,1280]{2,1,0:T(8,128)(2,1)S(1)} %pad_maximum_fusion.refs_1_), channel_id=1, source_target_pairs={{0,24},{8,16},{16,8},{24,0},{1,25},{9,17},{17,9},{25,1},{2,26},{10... | collective-permute-start | bytes 1474568 | tf_op jit(solution)/shard_map/ppermute | solution.py:732
  74.4 20.8 %collective-permute-start.17 = (bf16[4,48,1152]{2,1,0:T(8,128)(2,1)}, bf16[4,48,1152]{2,1,0:T(8,128)(2,1)}, u32[]{:S(2)}, u32[]{:S(2)}) collective-permute-start(bf16[4,48,1152]{2,1,0:T(8,128)(2,1)} %collective-permute-done.13.refs_2_), channel_id=1, source_target_pairs={{0,1},{1,0},{2,3},{3,2},{4,5},{5,4},{6,7},{7,6},{8,9},{9,8},{10,11... | collective-permute-start | bytes 1327112 | tf_op jit(solution)/shard_map/ppermute | solution.py:732
  74.4 20.8 %collective-permute-start.18 = (bf16[4,48,1152]{2,1,0:T(8,128)(2,1)}, bf16[4,48,1152]{2,1,0:T(8,128)(2,1)}, u32[]{:S(2)}, u32[]{:S(2)}) collective-permute-start(bf16[4,48,1152]{2,1,0:T(8,128)(2,1)} %collective-permute-done.14.refs_3_), channel_id=1, source_target_pairs={{0,1},{1,0},{2,3},{3,2},{4,5},{5,4},{6,7},{7,6},{8,9},{9,8},{10,11... | collective-permute-start | bytes 1327112 | tf_op jit(solution)/shard_map/ppermute | solution.py:732
  74.9 20.8 %collective-permute-start.19 = (bf16[4,48,1152]{2,1,0:T(8,128)(2,1)}, bf16[4,48,1152]{2,1,0:T(8,128)(2,1)}, u32[]{:S(2)}, u32[]{:S(2)}) collective-permute-start(bf16[4,48,1152]{2,1,0:T(8,128)(2,1)} %collective-permute-done.15.refs_4_), channel_id=1, source_target_pairs={{0,1},{1,0},{2,3},{3,2},{4,5},{5,4},{6,7},{7,6},{8,9},{9,8},{10,11... | collective-permute-start | bytes 1327112 | tf_op jit(solution)/shard_map/ppermute | solution.py:732
  94.7 20.7 %collective-permute-start.26 = (bf16[4,48,1280]{2,1,0:T(8,128)(2,1)S(1)}, bf16[4,48,1280]{2,1,0:T(8,128)(2,1)S(1)}, u32[]{:S(2)}, u32[]{:S(2)}) collective-permute-start(bf16[4,48,1280]{2,1,0:T(8,128)(2,1)S(1)} %pad_maximum_fusion.refs_1_), channel_id=1, source_target_pairs={{0,1},{1,0},{2,3},{3,2},{4,5},{5,4},{6,7},{7,6},{8,9},{9,8},{10,11... | collective-permute-start | bytes 1474568 | tf_op jit(solution)/shard_map/ppermute | solution.py:732
  94.7 20.7 %collective-permute-start.27 = (bf16[4,48,1280]{2,1,0:T(8,128)(2,1)}, bf16[4,48,1280]{2,1,0:T(8,128)(2,1)S(1)}, u32[]{:S(2)}, u32[]{:S(2)}) collective-permute-start(bf16[4,48,1280]{2,1,0:T(8,128)(2,1)} %collective-permute-done.23.refs_2_), channel_id=1, source_target_pairs={{0,1},{1,0},{2,3},{3,2},{4,5},{5,4},{6,7},{7,6},{8,9},{9,8},{10,11... | collective-permute-start | bytes 1474568 | tf_op jit(solution)/shard_map/ppermute | solution.py:732
  95.2 20.2 %collective-permute-start.28 = (bf16[4,48,1280]{2,1,0:T(8,128)(2,1)}, bf16[4,48,1280]{2,1,0:T(8,128)(2,1)S(1)}, u32[]{:S(2)}, u32[]{:S(2)}) collective-permute-start(bf16[4,48,1280]{2,1,0:T(8,128)(2,1)} %collective-permute-done.24.refs_3_), channel_id=1, source_target_pairs={{0,1},{1,0},{2,3},{3,2},{4,5},{5,4},{6,7},{7,6},{8,9},{9,8},{10,11... | collective-permute-start | bytes 1474568 | tf_op jit(solution)/shard_map/ppermute | solution.py:732
  95.2 20.1 %collective-permute-start.29 = (bf16[4,48,1280]{2,1,0:T(8,128)(2,1)}, bf16[4,48,1280]{2,1,0:T(8,128)(2,1)S(1)}, u32[]{:S(2)}, u32[]{:S(2)}) collective-permute-start(bf16[4,48,1280]{2,1,0:T(8,128)(2,1)} %collective-permute-done.25.refs_4_), channel_id=1, source_target_pairs={{0,1},{1,0},{2,3},{3,2},{4,5},{5,4},{6,7},{7,6},{8,9},{9,8},{10,11... | collective-permute-start | bytes 1474568 | tf_op jit(solution)/shard_map/ppermute | solution.py:732
  168.3 31.1 %collective-permute-start.40 = (bf16[16,48,1152]{2,1,0:T(8,128)(2,1)S(1)}, bf16[16,48,1152]{2,1,0:T(8,128)(2,1)S(1)}, u32[]{:S(2)}, u32[]{:S(2)}) collective-permute-start(bf16[16,48,1152]{2,1,0:T(8,128)(2,1)S(1)} %get-tuple-element.160), channel_id=1, source_target_pairs={{0,1},{1,0},{2,3},{3,2},{4,5},{5,4},{6,7},{7,6},{8,9},{9,8},{10,11... | collective-permute-start | bytes 5308424 | tf_op jit(solution)/shard_map/ppermute | solution.py:732
  179.3 21.1 %collective-permute-start.50 = (bf16[2,512,384]{2,1,0:T(8,128)(2,1)S(1)}, bf16[2,512,384]{2,1,0:T(8,128)(2,1)S(1)}, u32[]{:S(2)}, u32[]{:S(2)}) collective-permute-start(bf16[2,512,384]{2,1,0:T(8,128)(2,1)S(1)} %get-tuple-element.178), channel_id=1, source_target_pairs={{0,1},{1,0},{2,3},{3,2},{4,5},{5,4},{6,7},{7,6},{8,9},{9,8},{10,11... | collective-permute-start | bytes 2359304 | tf_op jit(solution)/shard_map/ppermute | solution.py:732
  208.3 21.6 %collective-permute-start.43 = (bf16[4,48,1152]{2,1,0:T(8,128)(2,1)S(1)}, bf16[4,48,1152]{2,1,0:T(8,128)(2,1)S(1)}, u32[]{:S(2)}, u32[]{:S(2)}) collective-permute-start(bf16[4,48,1152]{2,1,0:T(8,128)(2,1)S(1)} %get-tuple-element.164), channel_id=1, source_target_pairs={{0,24},{8,16},{16,8},{24,0},{1,25},{9,17},{17,9},{25,1},{2,26},{10... | collective-permute-start | bytes 1327112 | tf_op jit(solution)/shard_map/ppermute | solution.py:732
  209.8 22.7 %collective-permute-start.36 = (bf16[1,48,896]{2,1,0:T(8,128)(2,1)S(1)}, bf16[1,48,896]{2,1,0:T(8,128)(2,1)S(1)}, u32[]{:S(2)}, u32[]{:S(2)}) collective-permute-start(bf16[1,48,896]{2,1,0:T(8,128)(2,1)S(1)} %get-tuple-element.139), channel_id=1, source_target_pairs={{0,2},{2,0},{4,6},{6,4},{1,3},{3,1},{5,7},{7,5},{8,10},{10,8},{12,... | collective-permute-start | bytes 258056 | tf_op jit(solution)/shard_map/ppermute | solution.py:732
  210.2 22.8 %collective-permute-start.37 = (bf16[1,48,896]{2,1,0:T(8,128)(2,1)S(1)}, bf16[1,48,896]{2,1,0:T(8,128)(2,1)S(1)}, u32[]{:S(2)}, u32[]{:S(2)}) collective-permute-start(bf16[1,48,896]{2,1,0:T(8,128)(2,1)S(1)} %get-tuple-element.140), channel_id=1, source_target_pairs={{0,4},{2,6},{4,0},{6,2},{1,5},{3,7},{5,1},{7,3},{8,12},{10,14},{12... | collective-permute-start | bytes 258056 | tf_op jit(solution)/shard_map/ppermute | solution.py:732
  219.3 29.5 %collective-permute-start.52 = (bf16[5,48,512]{2,1,0:T(8,128)(2,1)S(1)}, bf16[5,48,512]{2,1,0:T(8,128)(2,1)S(1)}, u32[]{:S(2)}, u32[]{:S(2)}) collective-permute-start(bf16[5,48,512]{2,1,0:T(8,128)(2,1)S(1)} %get-tuple-element.190), channel_id=1, source_target_pairs={{0,8},{8,0},{16,24},{24,16},{1,9},{9,1},{17,25},{25,17},{2,10},{10... | collective-permute-start | bytes 737288 | tf_op jit(solution)/shard_map/ppermute | solution.py:732
  220.7 28.1 %collective-permute-start.53 = (bf16[5,48,512]{2,1,0:T(8,128)(2,1)S(1)}, bf16[5,48,512]{2,1,0:T(8,128)(2,1)S(1)}, u32[]{:S(2)}, u32[]{:S(2)}) collective-permute-start(bf16[5,48,512]{2,1,0:T(8,128)(2,1)S(1)} %get-tuple-element.191), channel_id=1, source_target_pairs={{0,16},{8,24},{16,0},{24,8},{1,17},{9,25},{17,1},{25,9},{2,18},{10... | collective-permute-start | bytes 737288 | tf_op jit(solution)/shard_map/ppermute | solution.py:732
  (94 other events, 1112.9 us)
where the time goes:
time: 294 us; the launch traced here: 289 us
  Pallas kernels  105 us (36%)
  starting transfers between devices  87 us (30%)
  waiting for transfers between devices  72.4 us (25%)
  local copies, waits for them, and re-layouts  14.1 us (5%)
  other arithmetic  5.91 us (2%)
    pallas_call x22, Pallas kernels, call(): pl.pallas_call(kernel, in_specs=[SMEM] + [in_space] * (len(inputs) - 1),...  105 us
    ppermute x62, starting transfers between devices, swap(): return lax.ppermute(x, axis, [(i, i ^ by) for i in range(size)])  81.3 us
    ppermute x62, waiting for transfers between devices, swap(): return lax.ppermute(x, axis, [(i, i ^ by) for i in range(size)])  70.8 us
  transfers between devices with their start and end apart: 65, of which 22 were waited for; matrix products, arithmetic and copies ran while one was open for 6% of the time, Pallas kernels for 20%

commit v1 on v0

--- a/solution.py
+++ b/solution.py
@@ -96,7 +96,7 @@
 SMEM = pl.BlockSpec(memory_space=pltpu.SMEM)
 ANY = pl.BlockSpec(memory_space=pl.ANY)
 CHUNK = 256
-AT_S, AT_Z, AT_C, AT_OWN, AT_LABEL = range(5)
+AT_S, AT_Z, AT_C, AT_OWN, AT_WHICH, AT_LABEL = range(6)
 
 
 def call(kernel, name, outs, inputs, estimate, scratch=(), limit=24, in_space=VMEM, out_spaces=None):
@@ -179,8 +179,8 @@
     inside = sublane((D, 1)) < PIXELS
     proj = jnp.where(inside, by_row[:D, :1], 0.0)
     base = sum(dot_tn(table, p) for p in parts(by_row, 3))[:, :1]
-    bases = dot_tn(table, embk_ref[...])
-    bases_sc[...] = jnp.where(first_of_four((D, D)), bases, 0.0).astype(BF16)
+    lane = lax.broadcasted_iota(jnp.int32, (D, D), 1)
+    bases_sc[...] = jnp.where(lane % 4 == 0, dot(emb, table), 0.0).astype(BF16)
     group = same_group()
     x_sc[...] = jnp.zeros_like(x_sc)
     x_sc[:PIXELS] = jnp.where(at_ref[AT_OWN] == 1, own_ref[...], got_ref[...])
@@ -195,15 +195,12 @@
         e = jnp.exp(scores - jnp.max(scores, axis=0, keepdims=True))
         agg = e * (4.0 / column_sum(e))
 
-        @pl.when(i < half // CHUNK)
-        def _():
-            agg_ref[:, here] = agg
-            x_ref[:, here] = packed
-
-        total = dot_tn((agg * x).astype(BF16), embk_ref[:D])
+        agg_ref[:, here] = agg
+        x_ref[:, here] = packed
+        total = dot(emb_ref[:, :D], (agg * x).astype(BF16))
         for p in parts(agg, 2):
-            total = total + dot_tn(p, bases_sc[...])
-        out_ref[here, :] = total.astype(BF16)
+            total = total + dot(bases_sc[...], p)
+        out_ref[here, :] = total.T.astype(BF16)
         return carry
 
     lax.fori_loop(0, tokens // CHUNK, step, 0)
@@ -216,12 +213,12 @@
         "embed",
         [
             ((tokens, D), BF16),
-            ((D, tokens // 2), F32),
-            ((D, tokens // 2), BF16),
+            ((D, tokens), F32),
+            ((D, tokens), BF16),
             ((ECOLS, D), BF16),
         ],
         [at, own, got, emb, vid4],
-        cost(3e9, 4e6, 4e5),
+        cost(2e9, 2e6),
         [pltpu.VMEM((D, tokens), BF16), pltpu.VMEM((D, D), BF16)],
     )
 
@@ -253,8 +250,8 @@
 
 
 def mod_row(mods_ref, at_ref, layer, index):
-    row = layer * GROUPS + at_ref[AT_LABEL]
-    return mods_ref[pl.ds(row, 1), D * index : D * (index + 1)]
+    row = 8 * (layer * GROUPS + at_ref[AT_LABEL]) + index
+    return mods_ref[pl.ds(row, 1), :D]
 
 
 def first_norm(h, mods_ref, at_ref, layer):
@@ -436,7 +433,7 @@
         "block_forward",
         [((count, D), BF16)] + kept,
         [at, h, mods, weights],
-        cost(6e9, 1.2e7, 3e6),
+        cost(2e9, 2e6),
         [pltpu.VMEM(shape, kind) for shape, kind in kept] + [pltpu.SemaphoreType.DMA((3, 7))],
         limit=28,
         out_spaces=[VMEM] + [ANY] * len(kept),
@@ -562,7 +559,7 @@
         ]
         + cut.shapes(HALF + 128),
         [at, h, q, own, other, mods, weights, truth, got, basis],
-        cost(1.2e10, 1.2e7, 4e6),
+        cost(4e9, 4e6),
         rows_scratch(count, [FF, FF, D, D, D, D, 512, 512])
         + [pltpu.VMEM((count, FF), F32), pltpu.VMEM((2, 256, 256), BF16)]
         + cut.scratch(HALF),
@@ -571,16 +568,19 @@
 
 
 def attention_back_kernel(
-    at_ref, q_ref, own_ref, other_ref, lse_ref, att_ref, datt_ref, dq_ref, dk_ref, dv_ref, send_ref,
-    dk_sc, dv_sc,
+    at_ref, q_ref, own_ref, other_ref, lse_ref, att_ref, datt_ref, *refs, start, steps, more, finish,
 ):
     zero = jnp.zeros((), BF16)
-    count = q_ref.shape[0]
-    dk_sc[...] = jnp.zeros_like(dk_sc)
-    dv_sc[...] = jnp.zeros_like(dv_sc)
+    count = own_ref.shape[0]
+    if more:
+        dk_in, dv_in, refs = refs[0], refs[1], refs[2:]
+    dq_ref, *outs = refs
+    dk_sc, dv_sc = outs[-2:] if finish else outs[:2]
+    dk_sc[...] = dk_in[...] if more else jnp.zeros_like(dk_sc)
+    dv_sc[...] = dv_in[...] if more else jnp.zeros_like(dv_sc)
 
     def step(i, carry):
-        rows = rows_at(i, CHUNK)
+        rows = rows_at(i + start, CHUNK)
         for pair in range(HEADS // 2):
             a = 128 * pair
             here = slice(a, a + 128)
@@ -602,57 +602,71 @@
                 d_q = d_q + dot(d_scores, k)
                 d_k = d_k + dot_tn(d_scores, jnp.where(mask, q, zero))
                 d_v = d_v + dot_tn(probs.astype(BF16), jnp.where(mask, d_att, zero))
-            dq_ref[rows, here] = (d_q * 0.125).astype(BF16)
+            dq_ref[rows_at(i, CHUNK), here] = (d_q * 0.125).astype(BF16)
             dk_sc[:, here] += d_k * 0.125
             dv_sc[:, here] += d_v
         return carry
 
-    lax.fori_loop(0, count // CHUNK, step, 0)
-    dk_ref[...] = dk_sc[:count]
-    dv_ref[...] = dv_sc[:count]
-    send_ref[0] = dk_sc[count:].astype(BF16)
-    send_ref[1] = dv_sc[count:].astype(BF16)
-
-
-def attention_back(at, q, own, other, lse, att, d_att):
+    lax.fori_loop(0, steps, step, 0)
+    if finish:
+        dk_ref, dv_ref, dk_send, dv_send = outs[:4]
+        dk_ref[...] = dk_sc[:count]
+        dv_ref[...] = dv_sc[:count]
+        dk_send[...] = dk_sc[count:].astype(BF16)
+        dv_send[...] = dv_sc[count:].astype(BF16)
+
+
+def attention_back(at, q, own, other, lse, att, d_att, start=0, steps=2, carried=(), finish=False):
     count = q.shape[0]
+    full = ((2 * count, D), F32)
+    outs = [((count, D), F32)] * 2 + [((count, D), BF16)] * 2 if finish else [full] * 2
+    options = dict(start=start, steps=steps, more=bool(carried), finish=finish)
     return call(
-        attention_back_kernel,
+        lambda *refs: attention_back_kernel(*refs, **options),
         "attention_back",
-        [((count, D), BF16), ((count, D), F32), ((count, D), F32), ((2, count, D), BF16)],
-        [at, q, own, other, lse, att, d_att],
-        cost(6e9, 8e6, 3e6),
-        [pltpu.VMEM((2 * count, D), F32)] * 2,
+        [((CHUNK * steps, D), BF16)] + outs,
+        [at, q, own, other, lse, att, d_att, *carried],
+        cost(1e9 * steps, 1e6),
+        [pltpu.VMEM(*full)] * 2 if finish else (),
     )
 
 
 def qkv_back(
-    at_ref, cut, outs, lane, layer, dq_ref, dk_ref, dv_ref, got_ref, h_ref, dmid_ref, gout_ref, mods_ref, w_ref,
+    at_ref, cut, outs, lane, layer, d_q, d_k, d_v, h_ref, dmid_ref, gout_ref, mods_ref, w_ref,
 ):
-    count = dq_ref.shape[0]
-    normed, x, inverse = first_norm(h_ref[:count], mods_ref, at_ref, layer)
-    d_k = (dk_ref[...] + got_ref[0].astype(F32)).astype(BF16)
-    d_v = (dv_ref[...] + got_ref[1].astype(F32)).astype(BF16)
-    d_n = jnp.zeros((count, D), F32)
-    for j, piece in enumerate((dq_ref[...], d_k, d_v)):
-        d_n = d_n + dot_nt(piece, w_ref[j, :, :D])
-        cut.write(at_ref, outs, j, lane, dot_tn(normed, piece))
+    count, rows = d_q.shape[0], d_k.shape[0]
+    normed, x, inverse = first_norm(h_ref[:rows], mods_ref, at_ref, layer)
+    first = dot_nt(d_q, w_ref[0, :, :D])
+    rest = dot_nt(d_k, w_ref[1, :, :D]) + dot_nt(d_v, w_ref[2, :, :D])
+    if rows > count:
+        d_n = jnp.concatenate([rest[:count] + first, rest[count:]], axis=0)
+    else:
+        d_n = rest + first
+    cut.write(at_ref, outs, 0, lane, dot_tn(normed[:count], d_q))
+    cut.write(at_ref, outs, 1, lane, dot_tn(normed, d_k))
+    cut.write(at_ref, outs, 2, lane, dot_tn(normed, d_v))
     cut.write(at_ref, outs, 3, lane, gout_ref[...])
     scale = 1.0 + mod_row(mods_ref, at_ref, layer, 1)
-    d_h = dmid_ref[...] + normal_back(d_n * scale, x, inverse)
+    d_h = normal_back(d_n * scale, x, inverse)
+    if rows > count:
+        d_h = jnp.concatenate([d_h[:count] + dmid_ref[...], d_h[count:]], axis=0)
+    else:
+        d_h = d_h + dmid_ref[...]
     return d_h.astype(BF16), column_sum(d_n), column_sum(d_n * x)
 
 
 def between_kernel(
-    at_ref, dq_ref, dk_ref, dv_ref, got_ref, h_ref, dmid_ref, gout_ref, dmod_ref, mods_ref, w1_ref,
+    at_ref, dq_ref, dk_ref, dv_ref, dk_got, dv_got, h_ref, dmid_ref, gout_ref, dmod_ref, mods_ref, w1_ref,
     one_ref, two_ref, mid_ref, slope_ref, act_ref, att_ref, w0_ref,
     dmid_out, datt_out, gout_out, dmod_out, dmod_next, keep_ref, send_ref,
     dh_sc, dunits_ref, dtwo_ref, n2_ref, done_ref, buffer, *, cut,
 ):
     outs = (keep_ref, send_ref)
     cut = cut.on(buffer)
+    d_k = (dk_ref[...] + dk_got[...].astype(F32)).astype(BF16)
+    d_v = (dv_ref[...] + dv_got[...].astype(F32)).astype(BF16)
     d_h, shift, scale = qkv_back(
-        at_ref, cut, outs, 0, 1, dq_ref, dk_ref, dv_ref, got_ref, h_ref, dmid_ref, gout_ref, mods_ref, w1_ref,
+        at_ref, cut, outs, 0, 1, dq_ref[...], d_k, d_v, h_ref, dmid_ref, gout_ref, mods_ref, w1_ref,
     )
     dmod_out[...] = dmod_ref[...]
     dmod_out[0:1] = shift
@@ -683,20 +697,22 @@
         [((count, D), F32), ((count, D), BF16), ((D, D), F32), ((8, D), F32), ((8, D), F32)]
         + cut.shapes(D + HALF),
         [at, *grads, h, d_mid, g_out, dmod, mods, w1, one, two, mid, slope, act, att, w0],
-        cost(6e9, 2e7),
+        cost(1e9, 1e6),
         rows_scratch(count, [D, FF, D, D, D]) + cut.scratch(HALF),
         limit=28,
     )
 
 
 def last_kernel(
-    at_ref, dq_ref, dk_ref, dv_ref, got_ref, h_ref, dmid_ref, gout_ref, dmod0_ref, dmod1_ref, loss_ref,
+    at_ref, dqa_ref, dqb_ref, dk_ref, dv_ref, h_ref, dmid_ref, gout_ref, dmod0_ref, dmod1_ref, loss_ref,
     mods_ref, w_ref, x_ref, agg_ref, embk_ref, vid_ref, keep_ref, send_ref, sums_sc, buffer, *, cut,
 ):
     outs = (keep_ref, send_ref)
     cut = cut.on(buffer)
+    d_q = jnp.concatenate([dqa_ref[...], dqb_ref[...]], axis=0)
+    d_k, d_v = dk_ref[...].astype(BF16), dv_ref[...].astype(BF16)
     d_h, shift, scale = qkv_back(
-        at_ref, cut, outs, 0, 0, dq_ref, dk_ref, dv_ref, got_ref, h_ref, dmid_ref, gout_ref, mods_ref, w_ref,
+        at_ref, cut, outs, 0, 0, d_q, d_k, d_v, h_ref, dmid_ref, gout_ref, mods_ref, w_ref,
     )
     sums_sc[...] = jnp.zeros_like(sums_sc)
     for group in range(GROUPS):
@@ -722,7 +738,7 @@
         "last",
         cut.shapes(ECOLS, True),
         [at, *grads, h, d_mid, g_out, dmod0, dmod1, loss, mods, w0, x, agg, embk, vid4],
-        cost(4e9, 1e7),
+        cost(1e9, 1e6),
         [pltpu.VMEM((48, ECOLS), F32)] + cut.scratch(D),
         limit=28,
     )
@@ -768,6 +784,84 @@
     )[0]
 
 
+def first_kernel(at_ref, own_ref, got_ref, emb_ref, mods_ref, out_ref):
+    rows = own_ref.shape[2]
+    total = jnp.zeros((rows, D), F32)
+    for jc, ref in enumerate((own_ref, got_ref)):
+        for jz in range(ref.shape[0]):
+            row = (at_ref[AT_Z] ^ jz) * 2 + (at_ref[AT_C] ^ jc)
+            emb_ref[rows_at(row, rows), :] = ref[jz, 0]
+            total = total + (ref[jz, 1, :, :D].astype(F32) + ref[jz, 2, :, :D].astype(F32))
+    mods_ref[...] = total
+    for i in range(AT_LABEL):
+        out_ref[i] = at_ref[i]
+    labels = jnp.where(
+        at_ref[AT_OWN] == 1, own_ref[0, 1, 0:8, 0:128].astype(F32), got_ref[0, 1, 0:8, 0:128].astype(F32)
+    )
+    picked = sublane((8, 128)) == 6 + at_ref[AT_WHICH]
+    out_ref[AT_LABEL] = jnp.max(jnp.where(picked, labels, 0.0)).astype(jnp.int32)
+
+
+def pack_kernel(
+    at_ref, labels_ref, emb_ref, qkv_ref, out_ref, up_ref, down_ref, ada_ref, head_ref,
+    first_ref, zero_ref, one_ref,
+):
+    rows = emb_ref.shape[0]
+    first_ref[...] = jnp.zeros_like(first_ref)
+    first_ref[0, :rows, :EROWS] = emb_ref[...].astype(BF16)
+    silu, _ = lead_parts(emb_ref)
+    for layer in range(LAYERS):
+        for i in range(6):
+            ada = ada_ref[layer, :, D * i : D * (i + 1)].astype(BF16).astype(F32)
+            for g in range(GROUPS):
+                at = 8 * (GROUPS * layer + g) + i
+                value = column_sum(silu[:, g : g + 1] * ada)
+                top = value.astype(BF16)
+                first_ref[1, at : at + 1, :D] = top
+                first_ref[2, at : at + 1, :D] = (value - top.astype(F32)).astype(BF16)
+    for i in range(2):
+        label = jnp.full((1, D), labels_ref[i], jnp.int32).astype(F32).astype(BF16)
+        first_ref[1, 6 + i : 7 + i, :D] = label
+    col = lax.broadcasted_iota(jnp.int32, (PIXELS, 128), 0)
+    lane = lax.broadcasted_iota(jnp.int32, (PIXELS, 128), 1)
+    for j in range(4):
+
+        def fill(j=j):
+            for layer, ref in enumerate((zero_ref, one_ref)):
+                at = 0 if ref.shape[0] == 1 else j
+                part = qkv_ref[layer, :, D * j : D * (j + 1)] if j < 3 else out_ref[layer]
+                ref[at, :, :D] = part.astype(BF16)
+                source = (up_ref if j < 2 else down_ref)[layer]
+                ref[at, :, D : 3 * D] = source[:, HALF * (j % 2) : HALF * (j % 2 + 1)].astype(BF16)
+            wide = lane + 128 * (j % 2)
+            pick = jnp.logical_and(col == 2 * wide + j // 2, wide < PIXELS // 2).astype(BF16)
+            at = 0 if one_ref.shape[0] == 1 else j
+            one_ref[at, :, 3 * D :] = dot(head_ref[...].astype(BF16), pick).astype(BF16)
+
+        if zero_ref.shape[0] == 4:
+            fill()
+        else:
+            pl.when(at_ref[AT_S] == j)(fill)
+
+
+def packed(at, labels, weights, quarters):
+    rows = weights[0].shape[0]
+    inputs = [at, labels, *weights]
+    return pl.pallas_call(
+        pack_kernel,
+        in_specs=[SMEM, SMEM] + [VMEM] * 7,
+        out_specs=[VMEM] * 3,
+        out_shape=[
+            jax.ShapeDtypeStruct((3, 48, ECOLS), BF16),
+            jax.ShapeDtypeStruct((quarters, rows, 3 * D), BF16),
+            jax.ShapeDtypeStruct((quarters, rows, 3 * D + 128), BF16),
+        ],
+        compiler_params=pltpu.CompilerParams(vmem_limit_bytes=16 << 20),
+        cost_estimate=cost(0, 1e6),
+        name="packed",
+    )(*inputs)
+
+
 def two_rows(v):
     loss = v[6:7] + v[7:8]
     top = loss.astype(BF16).astype(F32)
@@ -775,7 +869,18 @@
     return jnp.where(row == 6, top, jnp.where(row == 7, loss - top, v)).astype(BF16)
 
 
-def add_core_kernel(at_ref, kept_ref, got_ref, own_ref, *sends):
+class Rows:
+    def __init__(self, refs, cuts):
+        self.refs, self.cuts = refs, cuts
+
+    def fill(self, out):
+        for ref, a, b in zip(self.refs, self.cuts[:-1], self.cuts[1:]):
+            out[a:b] = ref[...]
+
+
+def add_core_kernel(at_ref, kept_ref, pieces, own_ref, *refs):
+    sends, got_ref = refs[:3], refs[3]
+    pieces.fill(got_ref)
     zs = 4
     for j in range(4):
         here = pl.ds((at_ref[AT_S] ^ j) * zs, zs)
@@ -818,6 +923,65 @@
         more[0][...] = summed(refs, 1)
 
 
+def add_split_kernel(at_ref, kept_ref, got_ref, own_ref, send_ref, *, by):
+    zs = 4
+    for i, j in enumerate((0, 3 - by, by, 3)):
+        here = pl.ds((at_ref[AT_S] ^ j) * zs, zs)
+        value = kept_ref[here].astype(F32) + got_ref[here].astype(F32)
+        if i < 2:
+            own_ref[i] = value
+        else:
+            send_ref[i - 2] = value.astype(BF16)
+
+
+def add_half_kernel(at_ref, own_ref, got_ref, kept_ref, send_ref):
+    kept_ref[...] = own_ref[0] + got_ref[0].astype(F32)
+    send_ref[...] = (own_ref[1] + got_ref[1].astype(F32)).astype(BF16)
+
+
+def add_quarter_kernel(at_ref, own_ref, got_ref, kept_ref, send_ref):
+    z = at_ref[AT_Z]
+    for i, j in enumerate((0, 2, 1, 3)):
+        value = own_ref[z ^ j] + got_ref[z ^ j].astype(F32)
+        if i < 2:
+            kept_ref[i] = value
+        else:
+            send_ref[i - 2] = value.astype(BF16)
+
+
+def add_both_kernel(at_ref, own_ref, got_ref, out_ref):
+    out_ref[...] = (own_ref[...] + got_ref[...].astype(F32)).astype(BF16)
+
+
+def both_split_kernel(at_ref, kept_ref, got_ref, owna_ref, ownb_ref, a_ref, b_ref):
+    for half, (own, send, by) in enumerate(((owna_ref, a_ref, 1), (ownb_ref, b_ref, 2))):
+        for i, j in enumerate((0, 3 - by, by, 3)):
+            here = pl.ds((at_ref[AT_S] ^ j) * 4 + 2 * half, 2)
+            value = kept_ref[here].astype(F32) + got_ref[here].astype(F32)
+            if i < 2:
+                own[i] = value
+            else:
+                send[i - 2] = value.astype(BF16)
+
+
+def both_half_kernel(at_ref, owna_ref, ownb_ref, gota_ref, gotb_ref, kept_ref, a_ref, b_ref):
+    for half, (own, got, send) in enumerate(((owna_ref, gota_ref, a_ref), (ownb_ref, gotb_ref, b_ref))):
+        kept_ref[2 * half : 2 * half + 2] = own[0] + got[0].astype(F32)
+        send[...] = (own[1] + got[1].astype(F32)).astype(BF16)
+
+
+def both_quarter_kernel(at_ref, own_ref, gota_ref, gotb_ref, kept_ref, *refs):
+    sends, sc = refs[:3], refs[3]
+    sc[0:2] = own_ref[0:2] + gota_ref[...].astype(F32)
+    sc[2:4] = own_ref[2:4] + gotb_ref[...].astype(F32)
+    for j in range(4):
+        value = sc[at_ref[AT_Z] ^ j]
+        if j == 0:
+            kept_ref[0] = value
+        else:
+            sends[j - 1][0] = value.astype(BF16)
+
+
 class Plain:
     split = False
 
@@ -825,24 +989,30 @@
         self.sizes, self.at = sizes, at
         self.order = at.at[AT_S].set(0)
 
-    def rows(self, x, ready):
-        return lax.all_gather(x, ("z", "c"), axis=0, tiled=True)
-
-    def columns(self, bundles, ready):
+    def first(self, x, labels, pairs):
+        rows = D // (2 * self.sizes["z"])
+        emb = lax.all_gather(x[0, :rows], ("z", "c"), axis=0, tiled=True)
+        mods = lax.psum(x[1].astype(F32) + x[2].astype(F32), ("z", "c"))
+        got = lax.ppermute(labels, CHIP, pairs)
+        label = jnp.where(self.at[AT_OWN] == 1, labels, got)[self.at[AT_WHICH]]
+        return emb, mods, self.at.at[AT_LABEL].set(label)
+
+    def columns(self, bundles):
         return [lax.all_gather(x, ("z", "c"), axis=1, tiled=True) for x in bundles]
 
     def total(self, x):
-        return lax.psum(x, ("z", "c"))
+        return lax.psum(x, ("z", "c")), jnp.zeros_like(x)
 
     def core(self, g):
         own = lax.psum_scatter(g[0].astype(F32), ("z", "c"), scatter_dimension=1, tiled=True)
         return lax.psum(own, "s"), lax.psum(g[1][0].astype(F32), CHIP)
 
+    core_halves = core_both = core
+
     def segment(self, x):
         return x
 
-    def plane(self, x):
-        return x
+    plane = halves_one = halves_two = both_one = both_two = segment
 
     def shared(self, xs):
         return [[x[0][j].astype(BF16) for j in range(4)] for x in xs]
@@ -857,32 +1027,98 @@
     def across(self, x, axis):
         return [swap(x, axis, 4, by) for by in (1, 2, 3)]
 
-    def rows(self, x, ready):
+    def first(self, x, labels, pairs):
         own = jnp.stack([x] + self.across(x, "z"))
-        return placed(self.at, [own], [swap(own, "c", 2, 1)])
-
-    def columns(self, bundles, ready):
+        self.ready = own
+        return call(
+            first_kernel,
+            "first",
+            [((D, ECOLS), BF16), ((48, D), F32), ((AT_LABEL + 1,), jnp.int32)],
+            [self.at, own, swap(own, "c", 2, 1)],
+            cost(0, 1e6),
+            out_spaces=[VMEM, VMEM, SMEM],
+        )
+
+    def columns(self, bundles):
         out, wait = [], ()
         for x in bundles:
-            mine = lax.dynamic_index_in_dim(x, self.at[AT_S], 0, keepdims=False)
-            stack = jnp.stack([mine] + self.across(after(mine, *wait), "z"))
-            own = [stack] + self.across(after(stack, *wait), "s")
+            mine = x[0]
+            stack = jnp.stack([mine] + self.across(after(mine, *wait[:1]), "z"))
+            pieces = self.across(after(stack, *wait[1:]), "s")
+            own = [stack] + pieces
             out.append((own, [swap(y, "c", 2, 1) for y in own]))
-            wait = (stack,)
+            wait = (stack, *pieces)
+        self.ready = out[0][0][0]
         return [placed(self.at, own, got) for own, got in out]
 
     def total(self, x):
         one, two, three = self.across(x, "z")
         x = (x + one) + (two + three)
-        return x + swap(x, "c", 2, 1)
+        return x, swap(x, "c", 2, 1)
+
+    def run(self, kernel, name, outs, inputs, scratch=()):
+        return call(kernel, name, outs, [self.at, *inputs], cost(0, 1e5), scratch)
 
     def core(self, g):
         kept, sent = g
         count, rows, width = kept.shape
         full = (4 + count % 4, rows, width)
-        return call(
-            add_core_kernel, "add_core", [(full, F32)] + [(full, BF16)] * 3,
-            [self.at, kept, swap(sent, "c", 2, 1)], cost(0, 8 * math.prod(kept.shape)),
+        cuts = (0, count // 3, 2 * (count // 3), count)
+        got = [swap(sent[a:b], "c", 2, 1) for a, b in zip(cuts[:-1], cuts[1:])]
+        outs = [(full, F32)] + [(full, BF16)] * 3
+        return self.run(
+            lambda at, kept, *refs: add_core_kernel(at, kept, Rows(refs[:3], cuts), *refs[3:]),
+            "add_core", outs, [kept, *got], [pltpu.VMEM(kept.shape, BF16)],
+        )
+
+    def core_halves(self, g):
+        kept, sent = g
+        count, rows, width = kept.shape
+        half = (2, 4, rows, width)
+        return self.run(
+            lambda *refs: add_split_kernel(*refs, by=1), "add_split", [(half, F32), (half, BF16)],
+            [kept, swap(sent, "c", 2, 1)],
+        )
+
+    def halves_one(self, x):
+        own, send = x
+        full = own.shape[1:]
+        outs = [(full, F32), (full, BF16)]
+        return self.run(add_half_kernel, "add_half", outs, [own, swap(send, "s", 4, 1)])
+
+    def halves_two(self, x):
+        own, send = x
+        part = (2,) + own.shape[1:]
+        outs = [(part, F32), (part, BF16)]
+        own, send = self.run(add_quarter_kernel, "add_quarter", outs, [own, swap(send, "s", 4, 2)])
+        one = own.shape[1:]
+        outs = [(one, F32), (one, BF16)]
+        own, send = self.run(add_half_kernel, "add_half", outs, [own, swap(send, "z", 4, 1)])
+        return self.run(add_both_kernel, "add_both", [(one, BF16)], [own, swap(send, "z", 4, 2)])
+
+    def core_both(self, g):
+        kept, sent = g
+        count, rows, width = kept.shape
+        part = (2, 2, rows, width)
+        return self.run(
+            both_split_kernel, "both_split", [(part, F32)] * 2 + [(part, BF16)] * 2,
+            [kept, swap(sent, "c", 2, 1)],
+        )
+
+    def both_one(self, x):
+        own_a, own_b, a, b = x
+        part = own_a.shape[1:]
+        return self.run(
+            both_half_kernel, "both_half", [((4,) + part[1:], F32)] + [(part, BF16)] * 2,
+            [own_a, own_b, swap(a, "s", 4, 1), swap(b, "s", 4, 2)],
+        )
+
+    def both_two(self, x):
+        own, a, b = x
+        one = (1,) + own.shape[1:]
+        return self.run(
+            both_quarter_kernel, "both_quarter", [(one, F32)] + [(one, BF16)] * 3,
+            [own, swap(a, "s", 4, 2), swap(b, "s", 4, 1)], [pltpu.VMEM(own.shape, F32)],
         )
 
     def segment(self, x):
@@ -892,7 +1128,7 @@
         got = [swap(y, "s", 4, j + 1) for j, y in enumerate(sends)]
         return call(
             add_segment_kernel, "add_segment", [(one, F32)] + [(one, BF16)] * 3,
-            [self.at, own, *got], cost(0, 12 * math.prod(own.shape)),
+            [self.at, own, *got], cost(0, 1e5),
         )
 
     def plane(self, x):
@@ -902,7 +1138,7 @@
         return call(
             add_plane_kernel, "add_plane",
             [((rows, width), BF16)] + [((rows, width), F32)] * (count - 1),
-            [self.at, own, *got], cost(0, 12 * math.prod(own.shape)),
+            [self.at, own, *got], cost(0, 1e5),
         )
 
     def shared(self, xs):
@@ -1068,28 +1304,24 @@
     )
 
 
-def layer_bundle(qkv, out, up, down_t, extra):
-    pieces = []
-    for j in range(4):
-        first = qkv[:, D * j : D * (j + 1)] if j < 3 else out
-        source = up if j < 2 else down_t
-        second = source[:, HALF * (j % 2) : HALF * (j % 2 + 1)]
-        row = [first, second] + ([extra[j]] if extra is not None else [])
-        pieces.append(jnp.concatenate(row, axis=-1))
-    return jnp.stack(pieces)
-
-
 def per_device(sizes, *arrays):
     (tiles_in, truth_in, labels, var_ids, basis) = arrays[:5]
     masters = arrays[5:12]
-    embed_w, qkv_w, out_w, up_w, down_w, ada_w, head_w = masters
     segments, dp = sizes["s"], sizes["z"] * 2
     micro = tiles_in.shape[0]
     assert segments == 2 * micro
     rows = D // dp
     s, z, c = (lax.axis_index(name) for name in CHIP)
     which, owner = s % micro, s // micro
-    is_owner = c == owner
+    at = jnp.stack([s, z, c, c == owner, which, 0]).astype(jnp.int32)
+    fast = segments == 4 and sizes["z"] == 4
+    move = (Squares if fast else Plain)(sizes, at)
+    cut = Cut(sizes["z"], rows, move.split)
+    views = []
+    for k in range(3):
+        w = list(arrays[5 + 7 * k : 12 + 7 * k])
+        w[0], w[4] = w[0].T, w[4].transpose(0, 2, 1)
+        views += w
 
     pairs = []
     for a in range(segments):
@@ -1097,82 +1329,50 @@
             base = (a * sizes["z"] + b) * 2
             pairs.append((base + a // micro, base + 1 - a // micro))
     pick = lambda x: lax.dynamic_index_in_dim(x, which, 0, keepdims=False).T
-    tiles, truth = pick(tiles_in), pick(truth_in)
+
+    first, *bundles = packed(at, labels, views[:7], 1 if fast else 4)
+    tiles = pick(tiles_in)
     tiles_got = lax.ppermute(tiles, CHIP, pairs)
-    label = jnp.where(is_owner, labels, lax.ppermute(labels, CHIP, pairs))
-    label = lax.dynamic_index_in_dim(label, which, 0, keepdims=False)
-    at = jnp.stack([s, z, c, is_owner, label]).astype(jnp.int32)
-    move = (Squares if segments == 4 and sizes["z"] == 4 else Plain)(sizes, at)
-    cut = Cut(sizes["z"], rows, move.split)
-
-    emb_t = jnp.pad(embed_w.astype(BF16).T, ((0, 0), (0, ECOLS - EROWS)))
-    down_t = down_w.astype(BF16).transpose(0, 2, 1)
-    wide = jnp.arange(512)
-    source = 2 * (wide % 256) + wide // 256
-    to_head = (jnp.arange(PIXELS)[:, None] == source[None]) & (wide % 256 < PIXELS // 2)[None]
-    head_b = dot(head_w.astype(BF16), to_head.astype(BF16)).astype(BF16)
-    head_b = [head_b[:, 128 * j : 128 * j + 128] for j in range(4)]
-    qkv_b, out_b, up_b = qkv_w.astype(BF16), out_w.astype(BF16), up_w.astype(BF16)
-    bundles = [
-        layer_bundle(qkv_b[l], out_b[l], up_b[l], down_t[l], head_b if l == 1 else None)
-        for l in range(LAYERS)
-    ]
-
-    emb = move.rows(emb_t, ())
-    w0, w1 = move.columns(bundles, ())
-
-    lead = embed_w[LEAD:].astype(BF16).astype(F32)
-    ada = ada_w.astype(BF16).astype(F32)
-    mods = jnp.einsum("gd,ldm->lgm", jax.nn.silu(lead), ada, precision=lax.Precision.HIGHEST)
-    mods = jnp.pad(mods.reshape(LAYERS * GROUPS, 6 * D), ((0, 2), (0, 0)))
-    mods = move.total(mods)
-
+    emb, mods, at = move.first(first, labels, pairs)
+    w0, w1 = move.columns(bundles)
+    truth = pick(truth_in)
+    truth_got = lax.ppermute(after(truth, tiles_got), CHIP, pairs)
     vid4 = jnp.pad(jnp.repeat(var_ids, 4), (0, D - PIXELS), constant_values=-1)[None].astype(
         jnp.int32
     )
-    h0, agg, x_own, embk = embed(at, tiles, tiles_got, emb, vid4)
-    h1, q0, own0, other0, att0, lse0, *kept = block_forward(at, h0, mods, w0)
+    h0, agg, x_all, embk = embed(at, tiles, tiles_got, emb, vid4)
+    h1, q0, own0, other0, att0, lse0, *kept = block_forward(after(at, truth_got), h0, mods, w0)
     q1, own1 = qkv_rows(at, h1, mods, w1)
     other1 = swap(own1, "c", 2, 1)
-    truth_got = lax.ppermute(after(truth, emb), CHIP, pairs)
     d_mid, d_att, att1, lse1, g_out, dmod1, loss, *g_first = turn(
         at, cut, h1, q1, own1, other1, mods, w1, truth, truth_got, basis, 1.0 / (micro * dp)
     )
-
-    def attention_grads(at, q, own, other, lse, att, d_att):
-        d_q, d_k, d_v, send = attention_back(at, q, own, other, lse, att, d_att)
-        return d_q, d_k, d_v, swap(send, "c", 2, 1)
-
-    grads = attention_grads(at, q1, own1, other1, lse1, att1, d_att)
-    first = move.core(g_first)
+    d_q, d_k, d_v, *sent = attention_back(at, q1, own1, other1, lse1, att1, d_att, finish=True)
+    got = [swap(x, "c", 2, 1) for x in sent]
+    first = move.core_halves(g_first)
     d_mid, d_att, g_out, dmod1, dmod0, *g_second = between(
-        after(at, *first), cut, grads, h1, d_mid, g_out, dmod1, mods, w1, [att0, *kept], w0
-    )
-    grads = attention_grads(at, q0, own0, other0, lse0, att0, d_att)
-    second = move.core(g_second)
-    first = move.segment(first)
+        after(at, *first), cut, [d_q, d_k, d_v, *got], h1, d_mid, g_out, dmod1, mods, w1, [att0, *kept], w0
+    )
+    saved = (q0, own0, other0, lse0, att0, d_att)
+    d_qa, d_k, d_v = attention_back(at, *saved, steps=1)
+    second = move.core_both(g_second)
+    first = move.halves_one(first)
+    d_qb, d_k, d_v = attention_back(
+        after(at, *second, *first), *saved, start=1, steps=1, carried=(d_k, d_v)
+    )
     g_third = last(
-        after(at, *second, *first), cut, grads, h0, d_mid, g_out, dmod0, dmod1, loss, mods, w0, x_own, agg, embk, vid4
-    )
-    third = move.core(g_third)
-    first = move.plane(first)
-    second = move.plane(move.segment(second))
+        at, cut, [d_qa, d_qb, d_k, d_v], h0, d_mid, g_out, dmod0, dmod1, loss, mods, w0, x_all, agg, embk, vid4
+    )
+    second = move.both_one(second)
+    third = move.core([g_third[0], after(g_third[1])])
     third = move.plane(move.segment(third))
+    first = move.halves_two(first)
+    second = move.plane(move.both_two(second))
     ends = move.shared([first, second]) + move.shared([third])
     sums = third[1]
 
-    views = []
-    for k in range(3):
-        w = list(arrays[5 + 7 * k : 12 + 7 * k])
-        w[0], w[4] = w[0].T, w[4].transpose(0, 2, 1)
-        views += w
     g1, g2, g3, lead_g, squares = gathered(move.order, ends, views[0], views[5], sums)
-    if move.split:
-        one, two, three = move.across(squares, "z")
-        own = (squares + one) + (two + three)
-        got = swap(own, "c", 2, 1)
-    else:
-        own, got = move.total(squares), jnp.zeros_like(squares)
+    own, got = move.total(squares)
     count = sum(w.size for w in masters) * dp
     rate = 0.02 * math.sqrt(count) / CLIP
     *new, loss_value, norm = updated(at, (g1, g2, g3), lead_g, sums, own, got, views, rate)

time: 294 us -> 275 us (0.935)
  starting transfers between devices: 87 us -> 69.4 us
  Pallas kernels: 105 us -> 111 us
  other arithmetic: 5.91 us -> 0.23 us
  local copies, waits for them, and re-layouts: 14.1 us -> 17.8 us
  waiting for transfers between devices: 72.4 us -> 68.9 us
    ppermute x62 -> x59, starting transfers between devices: 81.3 us -> 64 us  [swap(): return lax.ppermute(x, axis, [(i, i ^ by) for i in range(size)])]
    unnamed x108 -> x122, local copies, waits for them, and re-layouts: 3.12 us -> 15 us
    pallas_call x22 -> x26, Pallas kernels: 105 us -> 110 us  [call(): pl.pallas_call(kernel, in_specs=[SMEM] + [in_space] * (len(inputs) - 1),...]
    ppermute x62 -> x59, waiting for transfers between devices: 70.8 us -> 68.9 us  [swap(): return lax.ppermute(x, axis, [(i, i ^ by) for i in range(size)])]
  transfers between devices with their start and end apart: 65 -> 61, of which waited for: 22 -> 25; matrix products, arithmetic and copies ran while one was open for 6% -> 1% of each run, Pallas kernels for 20% -> 26%
where the time goes in v1:
time: 275 us; the launch traced here: 269 us
  Pallas kernels  111 us (40%)
  starting transfers between devices  69.4 us (25%)
  waiting for transfers between devices  68.9 us (25%)
  local copies, waits for them, and re-layouts  17.8 us (6%)
    pallas_call x26, Pallas kernels, call(): pl.pallas_call(kernel, in_specs=[SMEM] + [in_space] * (len(inputs) - 1),...  110 us
    ppermute x59, waiting for transfers between devices, swap(): return lax.ppermute(x, axis, [(i, i ^ by) for i in range(size)])  68.9 us
    ppermute x59, starting transfers between devices, swap(): return lax.ppermute(x, axis, [(i, i ^ by) for i in range(size)])  64 us
    unnamed x122, local copies, waits for them, and re-layouts  15 us
  transfers between devices with their start and end apart: 61, of which 25 were waited for; matrix products, arithmetic and copies ran while one was open for 1% of the time, Pallas kernels for 26%

profile of v1, /device:TPU:0, one launch (start us, length us, event | category | flops | bytes accessed | tf_op | source)
XLA Modules:
  0.0 269.5 jit_solution(12933569268951984317)
XLA Ops:
  9.7 5.1 %collective-permute-start.8 = (bf16[48,1152]{1,0:T(8,128)(2,1)S(1)}, bf16[48,1152]{1,0:T(8,128)(2,1)S(1)}, u32[]{:S(2)}, u32[]{:S(2)}) collective-permute-start(bf16[48,1152]{1,0:T(8,128)(2,1)S(1)} %bitcast.56), channel_id=1, source_target_pairs={{0,6},{2,4},{4,2},{6,0},{1,7},{3,5},{5,3},{7,1},{8,14},{10,12},{12... | collective-permute-start | bytes 331784 | tf_op jit(solution)/shard_map/ppermute | solution.py:748
  15.4 3.7 %collective-permute-start.2 = (bf16[3,48,512]{2,1,0:T(8,128)(2,1)S(1)}, bf16[3,48,512]{2,1,0:T(8,128)(2,1)S(1)}, u32[]{:S(2)}, u32[]{:S(2)}) collective-permute-start(bf16[3,48,512]{2,1,0:T(8,128)(2,1)S(1)} %get-tuple-element.138), channel_id=1, source_target_pairs={{0,6},{2,4},{4,2},{6,0},{1,7},{3,5},{5,3},{7,1},{8,14},{10,12},{12... | collective-permute-start | bytes 442376 | tf_op jit(solution)/shard_map/ppermute | solution.py:748
  19.2 4.9 %collective-permute-start = (bf16[3,48,512]{2,1,0:T(8,128)(2,1)S(1)}, bf16[3,48,512]{2,1,0:T(8,128)(2,1)S(1)}, u32[]{:S(2)}, u32[]{:S(2)}) collective-permute-start(bf16[3,48,512]{2,1,0:T(8,128)(2,1)S(1)} %get-tuple-element.138), channel_id=1, source_target_pairs={{0,2},{2,0},{4,6},{6,4},{1,3},{3,1},{5,7},{7,5},{8,10},{10,8},{12,... | collective-permute-start | bytes 442376 | tf_op jit(solution)/shard_map/ppermute | solution.py:748
  24.1 7.3 %collective-permute-done.7 = bf16[48,1152]{1,0:T(8,128)(2,1)S(1)} collective-permute-done((bf16[48,1152]{1,0:T(8,128)(2,1)S(1)}, bf16[48,1152]{1,0:T(8,128)(2,1)S(1)}, u32[]{:S(2)}, u32[]{:S(2)}) %collective-permute-start.7) | collective-permute-done | bytes 110624 | tf_op jit(solution)/shard_map/ppermute | solution.py:748
  39.3 5.0 %collective-permute-done.18 = bf16[48,1280]{1,0:T(8,128)(2,1)S(1)} collective-permute-done((bf16[48,1280]{1,0:T(8,128)(2,1)S(1)}, bf16[48,1280]{1,0:T(8,128)(2,1)S(1)}, u32[]{:S(2)}, u32[]{:S(2)}) %collective-permute-start.18) | collective-permute-done | bytes 122912 | tf_op jit(solution)/shard_map/ppermute | solution.py:748
  44.4 4.3 %collective-permute-start.16 = (bf16[48,1280]{1,0:T(8,128)(2,1)S(1)}, bf16[48,1280]{1,0:T(8,128)(2,1)S(1)}, u32[]{:S(2)}, u32[]{:S(2)}) collective-permute-start(bf16[48,1280]{1,0:T(8,128)(2,1)S(1)} %bitcast.55), channel_id=1, source_target_pairs={{0,2},{2,0},{4,6},{6,4},{1,3},{3,1},{5,7},{7,5},{8,10},{10,8},{12,... | collective-permute-start | bytes 368648 | tf_op jit(solution)/shard_map/ppermute | solution.py:748
  63.7 3.4 %collective-permute-start.5 = (bf16[276,1024]{1,0:T(8,128)(2,1)S(1)}, bf16[276,1024]{1,0:T(8,128)(2,1)}, u32[]{:S(2)}, u32[]{:S(2)}) collective-permute-start(bf16[276,1024]{1,0:T(8,128)(2,1)S(1)} %bitcast.48), channel_id=1, source_target_pairs={{0,1},{2,3},{4,5},{6,7},{8,9},{10,11},{12,13},{14,15},{17,16},{19,... | collective-permute-start | bytes 1695752 | tf_op jit(solution)/shard_map/ppermute | solution.py:1339
  70.6 11.3 %collective-permute-done.20.refs_3_ = bf16[4,48,1280]{2,1,0:T(8,128)(2,1)} collective-permute-done((bf16[4,48,1280]{2,1,0:T(8,128)(2,1)S(1)}, bf16[4,48,1280]{2,1,0:T(8,128)(2,1)}, u32[]{:S(2)}, u32[]{:S(2)}) %collective-permute-start.20) | collective-permute-done | bytes 491552 | tf_op jit(solution)/shard_map/ppermute | solution.py:748
  86.2 8.8 %embed.1 = (bf16[1024,384]{1,0:T(8,128)(2,1)S(1)}, f32[384,1024]{1,0:T(8,128)S(1)}, bf16[384,1024]{1,0:T(8,128)(2,1)S(1)}, bf16[512,384]{1,0:T(8,128)(2,1)S(1)}) custom-call(s32[6]{0:T(128)S(1)} %get-tuple-element.199.at_ref.refs_0_, bf16[276,1024]{1,0:T(8,128)(2,1)S(1)} %bitcast.51, bf16[276,1024]{1,0:T(8,128)(2,1)S(1)} %copy-done.56, ...), custom_call_target="tpu_custom_call" | custom-call | flops 2000000000 | bytes 2000000 | tf_op jit(solution)/shard_map/embed/pallas_call | solution.py:103
  95.1 5.3 %placed.2.w_ref.refs_18_.refs_12_ = bf16[4,384,1152]{2,1,0:T(8,128)(2,1)S(1)} custom-call(s32[6]{0:T(128)S(1)} %stack.66.at_ref.refs_0_.at, bf16[4,48,1152]{2,1,0:T(8,128)(2,1)S(1)} %pad_maximum_fusion.2.refs_1_, bf16[4,48,1152]{2,1,0:T(8,128)(2,1)S(1)} %copy-done.29, bf16[4,48,1152]{2,1,0:T(8,128)(2,1)} %collective-permute-done.10.refs_3_, ...), custom_call_target="tpu_custom_call" | custom-call | bytes 7077888 | tf_op jit(solution)/shard_map/placed/pallas_call | solution.py:103
  100.4 16.2 %block_forward.1 = (bf16[512,384]{1,0:T(8,128)(2,1)S(1)}, bf16[512,384]{1,0:T(8,128)(2,1)S(1)}, bf16[512,768]{1,0:T(8,128)(2,1)S(1)}, bf16[512,768]{1,0:T(8,128)...) custom-call(s32[6]{0:T(128)S(1)} %get-tuple-element.199.at_ref.refs_, ...), custom_call_target="tpu_custom_call" | custom-call | flops 2000000000 | bytes 2000000 | tf_op jit(solution)/shard_map/block_forward/pallas_call | solution.py:103
  116.7 3.5 %placed.3.w_ref.refs_6_.refs_11_ = bf16[4,384,1280]{2,1,0:T(8,128)(2,1)S(1)} custom-call(s32[6]{0:T(128)S(1)} %stack.66.at_ref.refs_0_.at, bf16[4,48,1280]{2,1,0:T(8,128)(2,1)S(1)} %pad_maximum_fusion.1.refs_1_, bf16[4,48,1280]{2,1,0:T(8,128)(2,1)} %collective-permute-done.19.refs_2_, bf16[4,48,1280]{2,1,0:T(8,128)(2,1)} %collective-permute-done.20.refs_3_, ...), custom_call_target="tpu_custom_call" | custom-call | bytes 7864320 | tf_op jit(solution)/shard_map/placed/pallas_call | solution.py:103
  124.6 20.9 %turn.1 = (f32[512,384]{1,0:T(8,128)S(1)}, bf16[512,384]{1,0:T(8,128)(2,1)S(1)}, bf16[512,384]{1,0:T(8,128)(2,1)S(1)}, f32[512,128]{1,0:T(8,128)S(1)}, f32[384,3...) custom-call(s32[6]{0:T(128)S(1)} %get-tuple-element.199.at_ref.refs_, ...), custom_call_target="tpu_custom_call" | custom-call | flops 4000000000 | bytes 4000000 | tf_op jit(solution)/shard_map/turn/pallas_call | solution.py:103
  145.6 10.9 %attention_back.3 = (bf16[512,384]{1,0:T(8,128)(2,1)S(1)}, f32[512,384]{1,0:T(8,128)S(1)}, f32[512,384]{1,0:T(8,128)S(1)}, bf16[512,384]{1,0:T(8,128)(2,1)S(1)}, bf16[512,384]{1,0:T(8,128)(2,1)S(1)}) custom-call(s32[6]{0:T(128)S(1)} %get-tuple-element.199.at_ref.refs_0_, bf16[512,384]{1,0:T(8,128)(2,1)S(1)} %get-tuple-element.150.refs_2_.refs_1_, ...), custom_call_target="tpu_custom_call" | custom-call | flops 2000000000 | bytes 1000000 | tf_op jit(solution)/shard_map/attention_back/pallas_call | solution.py:103
  158.9 7.0 %between.1 = (f32[512,384]{1,0:T(8,128)S(1)}, bf16[512,384]{1,0:T(8,128)(2,1)S(1)}, f32[384,384]{1,0:T(8,128)S(1)}, f32[8,384]{1,0:T(8,128)S(1)}, f32[8,384]{1,0...) custom-call(s32[6]{0:T(128)S(1)} %get-tuple-element.199.at_ref.refs_0_, ...), custom_call_target="tpu_custom_call" | custom-call | flops 1000000000 | bytes 1000000 | tf_op jit(solution)/shard_map/between/pallas_call | solution.py:103
  167.6 5.3 %attention_back.4 = (bf16[256,384]{1,0:T(8,128)(2,1)S(1)}, f32[1024,384]{1,0:T(8,128)S(1)}, f32[1024,384]{1,0:T(8,128)S(1)}) custom-call(s32[6]{0:T(128)S(1)} %get-tuple-element.199.at_ref.refs_0_, bf16[512,384]{1,0:T(8,128)(2,1)S(1)} %get-tuple-element.193.refs_1_, bf16[512,768]{1,0:T(8,128)(2,1)S(1)} %get-tuple-element.194.refs_2_, ...), custom_call_target="tpu_custom_call" | custom-call | flops 1000000000 | bytes 1000000 | tf_op jit(solution)/shard_map/attention_back/pallas_call | solution.py:103
  172.9 11.0 %collective-permute-done.28.got_ref = bf16[2,4,48,896]{3,2,1,0:T(8,128)(2,1)S(1)} collective-permute-done((bf16[2,4,48,896]{3,2,1,0:T(8,128)(2,1)S(1)}, bf16[2,4,48,896]{3,2,1,0:T(8,128)(2,1)S(1)}, u32[]{:S(2)}, u32[]{:S(2)}) %collective-permute-start.28) | collective-permute-done | bytes 688160 | tf_op jit(solution)/shard_map/ppermute | solution.py:748
  188.9 5.3 %attention_back.5 = (bf16[256,384]{1,0:T(8,128)(2,1)S(1)}, f32[1024,384]{1,0:T(8,128)S(1)}, f32[1024,384]{1,0:T(8,128)S(1)}) custom-call(s32[6]{0:T(128)S(1)} %get-tuple-element.199.at_ref.refs_0_, bf16[512,384]{1,0:T(8,128)(2,1)S(1)} %copy-done.45, bf16[512,768]{1,0:T(8,128)(2,1)S(1)} %copy-done.17, bf16[512,768]{1,0:T(8,128)(2,1)S(1)} %get-tuple-element.195.refs_3_, ...), custom_call_target="tpu_custom_call" | custom-call | flops 1000000000 | bytes 1000000 | tf_op jit(solution)/shard_map/attention_back/pallas_call | solution.py:103
  194.2 7.9 %last.1 = (bf16[17,48,512]{2,1,0:T(8,128)(2,1)S(1)}, bf16[17,48,512]{2,1,0:T(8,128)(2,1)S(1)}) custom-call(s32[6]{0:T(128)S(1)} %get-tuple-element.199.at_ref.refs_0_, bf16[256,384]{1,0:T(8,128)(2,1)S(1)} %get-tuple-element.198.refs_1_, bf16[256,384]{1,0:T(8,128)(2,1)S(1)} %get-tuple-element.202.refs_2_, f32[1024,384]{1,0:T(8,128)S(1)} %get-tuple-element.203.refs_3_, ...), custom_call_target="tpu_custom_call" | custom-call | flops 1000000000 | bytes 1000000 | tf_op jit(solution)/shard_map/last/pallas_call | solution.py:103
  215.5 5.7 %collective-permute-done.38.gotb_ref = bf16[2,48,1152]{2,1,0:T(8,128)(2,1)S(1)} collective-permute-done((bf16[2,48,1152]{2,1,0:T(8,128)(2,1)S(1)}, bf16[2,48,1152]{2,1,0:T(8,128)(2,1)S(1)}, u32[]{:S(2)}, u32[]{:S(2)}) %collective-permute-start.38) | collective-permute-done | bytes 221216 | tf_op jit(solution)/shard_map/ppermute | solution.py:748
  222.5 3.1 %collective-permute-start.40 = (bf16[1,48,1152]{2,1,0:T(8,128)(2,1)S(1)}, bf16[1,48,1152]{2,1,0:T(8,128)(2,1)S(1)}, u32[]{:S(2)}, u32[]{:S(2)}) collective-permute-start(bf16[1,48,1152]{2,1,0:T(8,128)(2,1)S(1)} %get-tuple-element.191), channel_id=1, source_target_pairs={{0,4},{2,6},{4,0},{6,2},{1,5},{3,7},{5,1},{7,3},{8,12},{10,14},{12... | collective-permute-start | bytes 331784 | tf_op jit(solution)/shard_map/ppermute | solution.py:748
  227.9 3.5 %collective-permute-done.40.b_ref = bf16[1,48,1152]{2,1,0:T(8,128)(2,1)S(1)} collective-permute-done((bf16[1,48,1152]{2,1,0:T(8,128)(2,1)S(1)}, bf16[1,48,1152]{2,1,0:T(8,128)(2,1)S(1)}, u32[]{:S(2)}, u32[]{:S(2)}) %collective-permute-start.40) | collective-permute-done | bytes 110624 | tf_op jit(solution)/shard_map/ppermute | solution.py:748
  242.3 3.6 %collective-permute-done.53.c_ref = bf16[2,48,512]{2,1,0:T(8,128)(2,1)S(1)} collective-permute-done((bf16[2,48,512]{2,1,0:T(8,128)(2,1)S(1)}, bf16[2,48,512]{2,1,0:T(8,128)(2,1)S(1)}, u32[]{:S(2)}, u32[]{:S(2)}) %collective-permute-start.53) | collective-permute-done | bytes 98336 | tf_op jit(solution)/shard_map/ppermute | solution.py:748
  263.8 5.5 %updated.1 = (f32[48,349]{1,0:T(8,128)}, f32[2,48,1152]{2,1,0:T(8,128)}, f32[2,48,384]{2,1,0:T(8,128)}, f32[2,48,1536]{2,1,0:T(8,128)}, f32[2,48,1536]{2,1,0:T(8...) custom-call(s32[6]{0:T(128)S(1)} %get-tuple-element.199.at_ref.refs_, ...), custom_call_target="tpu_custom_call" | custom-call | bytes 20000000 | tf_op jit(solution)/shard_map/updated/pallas_call | solution.py:103
  (267 shorter events, 98.9 us)
Async XLA Ops:
  14.8 16.6 %collective-permute-start.7 = (bf16[48,1152]{1,0:T(8,128)(2,1)S(1)}, bf16[48,1152]{1,0:T(8,128)(2,1)S(1)}, u32[]{:S(2)}, u32[]{:S(2)}) collective-permute-start(bf16[48,1152]{1,0:T(8,128)(2,1)S(1)} %bitcast.57), channel_id=1, source_target_pairs={{0,4},{2,6},{4,0},{6,2},{1,5},{3,7},{5,1},{7,3},{8,12},{10,14},{12... | collective-permute-start | bytes 331784 | tf_op jit(solution)/shard_map/ppermute | solution.py:748
  14.8 16.6 %collective-permute-start.6 = (bf16[48,1152]{1,0:T(8,128)(2,1)S(1)}, bf16[48,1152]{1,0:T(8,128)(2,1)S(1)}, u32[]{:S(2)}, u32[]{:S(2)}) collective-permute-start(bf16[48,1152]{1,0:T(8,128)(2,1)S(1)} %bitcast.58), channel_id=1, source_target_pairs={{0,2},{2,0},{4,6},{6,4},{1,3},{3,1},{5,7},{7,5},{8,10},{10,8},{12,... | collective-permute-start | bytes 331784 | tf_op jit(solution)/shard_map/ppermute | solution.py:748
  15.4 19.1 %collective-permute-start.2 = (bf16[3,48,512]{2,1,0:T(8,128)(2,1)S(1)}, bf16[3,48,512]{2,1,0:T(8,128)(2,1)S(1)}, u32[]{:S(2)}, u32[]{:S(2)}) collective-permute-start(bf16[3,48,512]{2,1,0:T(8,128)(2,1)S(1)} %get-tuple-element.138), channel_id=1, source_target_pairs={{0,6},{2,4},{4,2},{6,0},{1,7},{3,5},{5,3},{7,1},{8,14},{10,12},{12... | collective-permute-start | bytes 442376 | tf_op jit(solution)/shard_map/ppermute | solution.py:748
  19.2 17.6 %collective-permute-start.1 = (bf16[3,48,512]{2,1,0:T(8,128)(2,1)S(1)}, bf16[3,48,512]{2,1,0:T(8,128)(2,1)S(1)}, u32[]{:S(2)}, u32[]{:S(2)}) collective-permute-start(bf16[3,48,512]{2,1,0:T(8,128)(2,1)S(1)} %get-tuple-element.138), channel_id=1, source_target_pairs={{0,4},{2,6},{4,0},{6,2},{1,5},{3,7},{5,1},{7,3},{8,12},{10,14},{12... | collective-permute-start | bytes 442376 | tf_op jit(solution)/shard_map/ppermute | solution.py:748
  19.2 20.0 %collective-permute-start = (bf16[3,48,512]{2,1,0:T(8,128)(2,1)S(1)}, bf16[3,48,512]{2,1,0:T(8,128)(2,1)S(1)}, u32[]{:S(2)}, u32[]{:S(2)}) collective-permute-start(bf16[3,48,512]{2,1,0:T(8,128)(2,1)S(1)} %get-tuple-element.138), channel_id=1, source_target_pairs={{0,2},{2,0},{4,6},{6,4},{1,3},{3,1},{5,7},{7,5},{8,10},{10,8},{12,... | collective-permute-start | bytes 442376 | tf_op jit(solution)/shard_map/ppermute | solution.py:748
  31.5 22.0 %collective-permute-start.9 = (bf16[4,48,1152]{2,1,0:T(8,128)(2,1)S(1)}, bf16[4,48,1152]{2,1,0:T(8,128)(2,1)S(1)}, u32[]{:S(2)}, u32[]{:S(2)}) collective-permute-start(bf16[4,48,1152]{2,1,0:T(8,128)(2,1)S(1)} %pad_maximum_fusion.2.refs_1_), channel_id=1, source_target_pairs={{0,8},{8,0},{16,24},{24,16},{1,9},{9,1},{17,25},{25,17},{2,10},{10... | collective-permute-start | bytes 1327112 | tf_op jit(solution)/shard_map/ppermute | solution.py:748
  33.0 20.6 %collective-permute-start.10 = (bf16[4,48,1152]{2,1,0:T(8,128)(2,1)S(1)}, bf16[4,48,1152]{2,1,0:T(8,128)(2,1)}, u32[]{:S(2)}, u32[]{:S(2)}) collective-permute-start(bf16[4,48,1152]{2,1,0:T(8,128)(2,1)S(1)} %pad_maximum_fusion.2.refs_1_), channel_id=1, source_target_pairs={{0,16},{8,24},{16,0},{24,8},{1,17},{9,25},{17,1},{25,9},{2,18},{10... | collective-permute-start | bytes 1327112 | tf_op jit(solution)/shard_map/ppermute | solution.py:748
  34.5 20.3 %collective-permute-start.11 = (bf16[4,48,1152]{2,1,0:T(8,128)(2,1)S(1)}, bf16[4,48,1152]{2,1,0:T(8,128)(2,1)S(1)}, u32[]{:S(2)}, u32[]{:S(2)}) collective-permute-start(bf16[4,48,1152]{2,1,0:T(8,128)(2,1)S(1)} %pad_maximum_fusion.2.refs_1_), channel_id=1, source_target_pairs={{0,24},{8,16},{16,8},{24,0},{1,25},{9,17},{17,9},{25,1},{2,26},{10... | collective-permute-start | bytes 1327112 | tf_op jit(solution)/shard_map/ppermute | solution.py:748
  58.1 23.8 %collective-permute-start.20 = (bf16[4,48,1280]{2,1,0:T(8,128)(2,1)S(1)}, bf16[4,48,1280]{2,1,0:T(8,128)(2,1)}, u32[]{:S(2)}, u32[]{:S(2)}) collective-permute-start(bf16[4,48,1280]{2,1,0:T(8,128)(2,1)S(1)} %pad_maximum_fusion.1.refs_1_), channel_id=1, source_target_pairs={{0,16},{8,24},{16,0},{24,8},{1,17},{9,25},{17,1},{25,9},{2,18},{10... | collective-permute-start | bytes 1474568 | tf_op jit(solution)/shard_map/ppermute | solution.py:748
  59.5 22.5 %collective-permute-start.21 = (bf16[4,48,1280]{2,1,0:T(8,128)(2,1)S(1)}, bf16[4,48,1280]{2,1,0:T(8,128)(2,1)}, u32[]{:S(2)}, u32[]{:S(2)}) collective-permute-start(bf16[4,48,1280]{2,1,0:T(8,128)(2,1)S(1)} %pad_maximum_fusion.1.refs_1_), channel_id=1, source_target_pairs={{0,24},{8,16},{16,8},{24,0},{1,25},{9,17},{17,9},{25,1},{2,26},{10... | collective-permute-start | bytes 1474568 | tf_op jit(solution)/shard_map/ppermute | solution.py:748
  63.7 36.7 %collective-permute-start.5 = (bf16[276,1024]{1,0:T(8,128)(2,1)S(1)}, bf16[276,1024]{1,0:T(8,128)(2,1)}, u32[]{:S(2)}, u32[]{:S(2)}) collective-permute-start(bf16[276,1024]{1,0:T(8,128)(2,1)S(1)} %bitcast.48), channel_id=1, source_target_pairs={{0,1},{2,3},{4,5},{6,7},{8,9},{10,11},{12,13},{14,15},{17,16},{19,... | collective-permute-start | bytes 1695752 | tf_op jit(solution)/shard_map/ppermute | solution.py:1339
  67.9 48.8 %collective-permute-start.22 = (bf16[4,48,1280]{2,1,0:T(8,128)(2,1)S(1)}, bf16[4,48,1280]{2,1,0:T(8,128)(2,1)}, u32[]{:S(2)}, u32[]{:S(2)}) collective-permute-start(bf16[4,48,1280]{2,1,0:T(8,128)(2,1)S(1)} %pad_maximum_fusion.1.refs_1_), channel_id=1, source_target_pairs={{0,1},{1,0},{2,3},{3,2},{4,5},{5,4},{6,7},{7,6},{8,9},{9,8},{10,11... | collective-permute-start | bytes 1474568 | tf_op jit(solution)/shard_map/ppermute | solution.py:748
  70.6 46.1 %collective-permute-start.23 = (bf16[4,48,1280]{2,1,0:T(8,128)(2,1)}, bf16[4,48,1280]{2,1,0:T(8,128)(2,1)}, u32[]{:S(2)}, u32[]{:S(2)}) collective-permute-start(bf16[4,48,1280]{2,1,0:T(8,128)(2,1)} %collective-permute-done.19.refs_2_), channel_id=1, source_target_pairs={{0,1},{1,0},{2,3},{3,2},{4,5},{5,4},{6,7},{7,6},{8,9},{9,8},{10,11... | collective-permute-start | bytes 1474568 | tf_op jit(solution)/shard_map/ppermute | solution.py:748
  81.9 34.7 %collective-permute-start.24 = (bf16[4,48,1280]{2,1,0:T(8,128)(2,1)}, bf16[4,48,1280]{2,1,0:T(8,128)(2,1)}, u32[]{:S(2)}, u32[]{:S(2)}) collective-permute-start(bf16[4,48,1280]{2,1,0:T(8,128)(2,1)} %collective-permute-done.20.refs_3_), channel_id=1, source_target_pairs={{0,1},{1,0},{2,3},{3,2},{4,5},{5,4},{6,7},{7,6},{8,9},{9,8},{10,11... | collective-permute-start | bytes 1474568 | tf_op jit(solution)/shard_map/ppermute | solution.py:748
  81.9 34.7 %collective-permute-start.25 = (bf16[4,48,1280]{2,1,0:T(8,128)(2,1)}, bf16[4,48,1280]{2,1,0:T(8,128)(2,1)}, u32[]{:S(2)}, u32[]{:S(2)}) collective-permute-start(bf16[4,48,1280]{2,1,0:T(8,128)(2,1)} %collective-permute-done.21.refs_4_), channel_id=1, source_target_pairs={{0,1},{1,0},{2,3},{3,2},{4,5},{5,4},{6,7},{7,6},{8,9},{9,8},{10,11... | collective-permute-start | bytes 1474568 | tf_op jit(solution)/shard_map/ppermute | solution.py:748
  166.0 19.8 %collective-permute-start.34 = (bf16[16,48,1152]{2,1,0:T(8,128)(2,1)S(1)}, bf16[16,48,1152]{2,1,0:T(8,128)(2,1)S(1)}, u32[]{:S(2)}, u32[]{:S(2)}) collective-permute-start(bf16[16,48,1152]{2,1,0:T(8,128)(2,1)S(1)} %get-tuple-element.181), channel_id=1, source_target_pairs={{0,1},{1,0},{2,3},{3,2},{4,5},{5,4},{6,7},{7,6},{8,9},{9,8},{10,11... | collective-permute-start | bytes 5308424 | tf_op jit(solution)/shard_map/ppermute | solution.py:748
  166.4 17.5 %collective-permute-start.28 = (bf16[2,4,48,896]{3,2,1,0:T(8,128)(2,1)S(1)}, bf16[2,4,48,896]{3,2,1,0:T(8,128)(2,1)S(1)}, u32[]{:S(2)}, u32[]{:S(2)}) collective-permute-start(bf16[2,4,48,896]{3,2,1,0:T(8,128)(2,1)S(1)} %get-tuple-element.155), channel_id=1, source_target_pairs={{0,8},{8,0},{16,24},{24,16},{1,9},{9,1},{17,25},{25,17},{2,10},{10... | collective-permute-start | bytes 2064392 | tf_op jit(solution)/shard_map/ppermute | solution.py:748
  184.6 18.2 %collective-permute-start.29 = (bf16[4,48,896]{2,1,0:T(8,128)(2,1)S(1)}, bf16[4,48,896]{2,1,0:T(8,128)(2,1)S(1)}, u32[]{:S(2)}, u32[]{:S(2)}) collective-permute-start(bf16[4,48,896]{2,1,0:T(8,128)(2,1)S(1)} %get-tuple-element.157), channel_id=1, source_target_pairs={{0,16},{8,24},{16,0},{24,8},{1,17},{9,25},{17,1},{25,9},{2,18},{10... | collective-permute-start | bytes 1032200 | tf_op jit(solution)/shard_map/ppermute | solution.py:748
  186.7 16.8 %collective-permute-start.35 = (bf16[2,2,48,1152]{3,2,1,0:T(8,128)(2,1)S(1)}, bf16[2,2,48,1152]{3,2,1,0:T(8,128)(2,1)S(1)}, u32[]{:S(2)}, u32[]{:S(2)}) collective-permute-start(bf16[2,2,48,1152]{3,2,1,0:T(8,128)(2,1)S(1)} %get-tuple-element.184), channel_id=1, source_target_pairs={{0,8},{8,0},{16,24},{24,16},{1,9},{9,1},{17,25},{25,17},{2,10},{10... | collective-permute-start | bytes 1327112 | tf_op jit(solution)/shard_map/ppermute | solution.py:748
  187.3 17.7 %collective-permute-start.36 = (bf16[2,2,48,1152]{3,2,1,0:T(8,128)(2,1)S(1)}, bf16[2,2,48,1152]{3,2,1,0:T(8,128)(2,1)S(1)}, u32[]{:S(2)}, u32[]{:S(2)}) collective-permute-start(bf16[2,2,48,1152]{3,2,1,0:T(8,128)(2,1)S(1)} %get-tuple-element.185), channel_id=1, source_target_pairs={{0,16},{8,24},{16,0},{24,8},{1,17},{9,25},{17,1},{25,9},{2,18},{10... | collective-permute-start | bytes 1327112 | tf_op jit(solution)/shard_map/ppermute | solution.py:748
  207.6 18.0 %collective-permute-start.48 = (bf16[5,48,512]{2,1,0:T(8,128)(2,1)S(1)}, bf16[5,48,512]{2,1,0:T(8,128)(2,1)S(1)}, u32[]{:S(2)}, u32[]{:S(2)}) collective-permute-start(bf16[5,48,512]{2,1,0:T(8,128)(2,1)S(1)} %get-tuple-element.216), channel_id=1, source_target_pairs={{0,8},{8,0},{16,24},{24,16},{1,9},{9,1},{17,25},{25,17},{2,10},{10... | collective-permute-start | bytes 737288 | tf_op jit(solution)/shard_map/ppermute | solution.py:748
  209.7 17.3 %collective-permute-start.49 = (bf16[5,48,512]{2,1,0:T(8,128)(2,1)S(1)}, bf16[5,48,512]{2,1,0:T(8,128)(2,1)S(1)}, u32[]{:S(2)}, u32[]{:S(2)}) collective-permute-start(bf16[5,48,512]{2,1,0:T(8,128)(2,1)S(1)} %get-tuple-element.217), channel_id=1, source_target_pairs={{0,16},{8,24},{16,0},{24,8},{1,17},{9,25},{17,1},{25,9},{2,18},{10... | collective-permute-start | bytes 737288 | tf_op jit(solution)/shard_map/ppermute | solution.py:748
  210.9 16.1 %collective-permute-start.50 = (bf16[5,48,512]{2,1,0:T(8,128)(2,1)S(1)}, bf16[5,48,512]{2,1,0:T(8,128)(2,1)S(1)}, u32[]{:S(2)}, u32[]{:S(2)}) collective-permute-start(bf16[5,48,512]{2,1,0:T(8,128)(2,1)S(1)} %get-tuple-element.218), channel_id=1, source_target_pairs={{0,24},{8,16},{16,8},{24,0},{1,25},{9,17},{17,9},{25,1},{2,26},{10... | collective-permute-start | bytes 737288 | tf_op jit(solution)/shard_map/ppermute | solution.py:748
  234.1 16.0 %collective-permute-start.43 = (bf16[48,2048]{1,0:T(8,128)(2,1)S(1)}, bf16[48,2048]{1,0:T(8,128)(2,1)S(1)}, u32[]{:S(2)}, u32[]{:S(2)}) collective-permute-start(bf16[48,2048]{1,0:T(8,128)(2,1)S(1)} %pad_maximum_fusion.3), channel_id=1, source_target_pairs={{0,16},{8,24},{16,0},{24,8},{1,17},{9,25},{17,1},{25,9},{2,18},{10... | collective-permute-start | bytes 589832 | tf_op jit(solution)/shard_map/ppermute | solution.py:748
  (97 other events, 1291.5 us)
